TPU v7x, 512 devices: a whole 4x4x16 slice. The times are simulated.
512 devices in a mesh: dp: 128 (over z_lo, x, y, core), section: 4 (over z_hi).
Axes of the slice: x: 4, y: 4, z: 16 (z_hi: 4, z_lo: 4; z = z_hi * 4 + z_lo), core: 2. Of those that a mesh axis runs over, the one named last changes fastest.
Arguments:
- saved_inputs: bfloat16 [4, 2, 768, 6144], P('section', None, 'dp'), may hold values from -6 to 6
- carried: bfloat16 [4, 768, 6144], P('section', 'dp'), may hold values from -6 to 6
- head_grad: bfloat16 [768, 6144], P('dp'), may hold values from -6 to 6
- routing: int32 [4, 2, 768, 2], P('section', None, 'dp'), may hold values from 0 to 7, as said below
- replica_counts: int32 [128], replicated, may hold values from 2 to 5
- router: float32 [4, 6144, 8], P('section'), may hold values from -0.21875 to 0.21875
- w_in: bfloat16 [4, 128, 1536, 256], P('section', 'dp'), may hold values from -0.078125 to 0.078125
- w_out: bfloat16 [4, 128, 256, 1536], P('section', 'dp'), may hold values from -0.0625 to 0.0625
Outputs:
- input_grad: bfloat16 [2, 4, 768, 6144], P(None, 'section', 'dp')
- grad_in: bfloat16 [4, 128, 1536, 256], P('section', 'dp')
- grad_out: bfloat16 [4, 128, 256, 1536], P('section', 'dp')
- grad_router: float32 [4, 6144, 8], P('section')
Inputs may be any that keep to these rules, and one draw needn't show every extreme that they name: `routing`: each row names 2 different experts; in every section and step at most 2 of one device's 6 tokens name expert 0, and exactly 2 on some device.
All inputs are finite; a program needn't handle non-finite values.
Results may differ from a plain program's by a relative error of at most 0.0057.
Values may be sent and summed in bfloat16 or wider, within the bound.
A program may use at most 64 MiB of HBM per device.

v0:
```python
import jax
import jax.numpy as jnp
from jax import lax
from jax.sharding import PartitionSpec as P

STEPS = 2
CAP = 2


def shifted(array, axis, by):
    devices = lax.axis_size(axis)
    pairs = [(i, i + by) for i in range(devices) if 0 <= i + by < devices]
    return lax.ppermute(array, axis, pairs)


def from_partner(block, axis, distance):
    count = lax.axis_size(axis)
    route = []
    for low in range(count):
        high = low | 1 << distance
        if high != low and high < count:
            route += [(low, high), (high, low)]
    return lax.ppermute(block, axis, route)


def silu_grad(value):
    sig = jax.nn.sigmoid(value)
    return sig * (1.0 + value * (1.0 - sig))


def local(saved_inputs, carried, head_grad, routing, replica_counts, router, w_in, w_out):
    hi = lax.Precision.HIGHEST
    section_count = lax.axis_size("section")
    section_index = lax.axis_index("section")
    dev_count = lax.axis_size("dp")
    dev_index = lax.axis_index("dp")
    groups = dev_count // 4
    width = head_grad.shape[1]
    part = w_in.shape[2]
    hidden = w_in.shape[3]
    experts = router.shape[2]
    rows = dev_count * CAP
    weight_in = w_in[0, 0]
    weight_out = w_out[0, 0]
    router_w = router[0]
    quarter = dev_index % 4
    my_count = replica_counts[dev_index]
    first = (jnp.arange(experts) == 0).astype(jnp.float32)
    slots = jnp.arange(CAP, dtype=jnp.int32)

    def prepare(step):
        xin = saved_inputs[0, step]
        ids = routing[0, step]
        live = step + section_index < my_count
        xf = xin.astype(jnp.float32)
        logits = jnp.dot(xf, router_w, precision=hi)
        expo = jnp.exp(logits)
        prob = expo / jnp.sum(expo, axis=1, keepdims=True)
        routed = ((ids[:, 0] == 0) | (ids[:, 1] == 0)) & live
        flags = routed.astype(jnp.int32)
        slot = jnp.cumsum(flags, dtype=jnp.int32) - 1
        table = ((slot[None, :] == slots[:, None]) & routed[None, :]).astype(jnp.float32)
        xs = jnp.dot(table.astype(jnp.bfloat16), xin, preferred_element_type=jnp.float32).astype(
            jnp.bfloat16
        )
        gate = jnp.dot(table, prob[:, 0], precision=hi).astype(jnp.bfloat16)
        xsend = jnp.broadcast_to(
            xs.reshape(CAP, 4, part).transpose(1, 0, 2)[None], (groups, 4, CAP, part)
        ).reshape(dev_count, CAP, part)
        gsend = jnp.broadcast_to(gate[None], (dev_count, CAP))
        return (xf, prob, table, live, xsend, gsend)

    prepared = [prepare(step) for step in range(STEPS)]
    acc_in = jnp.zeros((part, hidden), jnp.float32)
    acc_out = jnp.zeros((hidden, part), jnp.float32)
    acc_router = jnp.zeros((width, experts), jnp.float32)
    outputs = []
    incoming = carried[0]
    for step in range(STEPS):
        xf, prob, table, live, xsend, gsend = prepared[step]
        if step == 1:
            passed = shifted(outputs[0], "section", -1)
            incoming = jnp.where(section_index == section_count - 1, head_grad, passed)
        grad_in_tok = jnp.where(live, incoming, jnp.zeros_like(incoming))
        ys = jnp.dot(
            table.astype(jnp.bfloat16), grad_in_tok, preferred_element_type=jnp.float32
        ).astype(jnp.bfloat16)
        ysend = jnp.broadcast_to(
            ys.reshape(CAP, 4, part).transpose(1, 0, 2)[None], (groups, 4, CAP, part)
        ).reshape(dev_count, CAP, part)
        recv_x, recv_y, recv_g = (
            lax.all_to_all(xsend, "dp", split_axis=0, concat_axis=0, tiled=True),
            lax.all_to_all(ysend, "dp", split_axis=0, concat_axis=0, tiled=True),
            lax.all_to_all(gsend, "dp", split_axis=0, concat_axis=0, tiled=True),
        )
        rows_x = recv_x.reshape(rows, part)
        rows_y = recv_y.reshape(rows, part)
        gate_f = recv_g.reshape(rows).astype(jnp.float32)[:, None]
        pre = jnp.dot(rows_x, weight_in, preferred_element_type=jnp.float32)
        upper = lax.dot_general(
            rows_y, weight_out, (((1,), (1,)), ((), ())), preferred_element_type=jnp.float32
        )
        for bit in range(2):
            other_pre, other_upper = from_partner((pre, upper), "dp", bit)
            pre = pre + other_pre
            upper = upper + other_upper
        act = jax.nn.silu(pre)
        dpre = (gate_f * upper * silu_grad(pre)).astype(jnp.bfloat16)
        scaled = (gate_f * act).astype(jnp.bfloat16)
        block_sum = jnp.sum(act * upper, axis=1)
        block_sum = jnp.where(quarter == 0, block_sum, jnp.zeros_like(block_sum)).astype(
            jnp.bfloat16
        )
        acc_in = acc_in + lax.dot_general(
            rows_x, dpre, (((0,), (0,)), ((), ())), preferred_element_type=jnp.float32
        )
        acc_out = acc_out + lax.dot_general(
            scaled, rows_y, (((0,), (0,)), ((), ())), preferred_element_type=jnp.float32
        )
        dx_part = lax.dot_general(
            dpre, weight_in, (((1,), (1,)), ((), ())), preferred_element_type=jnp.float32
        ).astype(jnp.bfloat16)
        back_x, back_g = (
            lax.all_to_all(
                dx_part.reshape(dev_count, CAP, part), "dp", split_axis=0, concat_axis=0, tiled=True
            ),
            lax.all_to_all(
                block_sum.reshape(dev_count, CAP), "dp", split_axis=0, concat_axis=0, tiled=True
            ),
        )
        summed = jnp.sum(back_x.astype(jnp.float32).reshape(groups, 4, CAP, part), axis=0)
        dxs = summed.transpose(1, 0, 2).reshape(CAP, width)
        dgate = jnp.sum(back_g.astype(jnp.float32), axis=0)
        dxe = lax.dot_general(table, dxs, (((0,), (0,)), ((), ())), precision=hi)
        dg_tok = lax.dot_general(table, dgate, (((0,), (0,)), ((), ())), precision=hi)
        dlog = (dg_tok * prob[:, 0])[:, None] * (first[None, :] - prob)
        result = grad_in_tok.astype(jnp.float32) + dxe + jnp.dot(dlog, router_w.T, precision=hi)
        outputs.append(result.astype(jnp.bfloat16))
        router_term = jnp.dot(xf.T, dlog, precision=hi)
        acc_router = acc_router + lax.psum(router_term, "dp")
    input_grad = jnp.stack(outputs)[:, None]
    grad_in = acc_in.astype(jnp.bfloat16)[None, None]
    grad_out = acc_out.astype(jnp.bfloat16)[None, None]
    return (input_grad, grad_in, grad_out, acc_router[None])


def solution(mesh):
    in_specs = (
        P("section", None, "dp", None),
        P("section", "dp", None),
        P("dp", None),
        P("section", None, "dp", None),
        P(),
        P("section", None, None),
        P("section", "dp", None, None),
        P("section", "dp", None, None),
    )
    out_specs = (
        P(None, "section", "dp", None),
        P("section", "dp", None, None),
        P("section", "dp", None, None),
        P("section", None, None),
    )
    return jax.shard_map(local, mesh=mesh, in_specs=in_specs, out_specs=out_specs, check_vma=False)
```

profile of v0, /device:TPU:1, one launch (start us, length us, event | category | flops | bytes accessed | tf_op | source)
XLA Modules:
  0.0 1497.2 jit_solution(10897805153019167695)
XLA Ops:
  10.7 1.9 fusion.54
  14.2 13.8 all-to-all-start.2
  28.2 23.6 %all-to-all-done.2 = bf16[128,2,1536]{2,1,0:T(2,128)(2,1)S(1)} async-done(((bf16[128,2,1536]{2,1,0:T(2,128)(2,1)}), bf16[128,2,1536]{2,1,0:T(2,128)(2,1)S(1)}, u32[]{:S(2)}, u32[]{:S(2)}) %all-to-all-start.2) | async-done | bytes 786464 | tf_op jit(solution)/shard_map/all_to_all | solution.py:92
  53.1 7.4 all-to-all-start.1
  62.5 3.0 collective-permute-start.2
  65.4 18.8 %all-to-all-done.1 = bf16[128,2,1536]{2,1,0:T(2,128)(2,1)} async-done(((bf16[128,2,1536]{2,1,0:T(2,128)(2,1)}), bf16[128,2,1536]{2,1,0:T(2,128)(2,1)}, u32[]{:S(2)}, u32[]{:S(2)}) %all-to-all-start.1) | async-done | bytes 786464 | tf_op jit(solution)/shard_map/all_to_all | solution.py:93
  84.2 2.3 reshape.242
  86.9 3.1 collective-permute-start
  91.3 1.9 collective-permute-start.3
  93.3 3.4 collective-permute-start.1
  97.5 5.7 all-to-all-start
  103.2 10.1 all-to-all-done
  115.2 1.8 multiply_reduce_fusion.1
  117.8 6.4 all-to-all-start.4
  126.7 7.6 all-to-all-done.4
  134.3 5.9 all-to-all-start.3
  142.2 1.4 reduce-window.17
  145.5 1.7 convolution_convert_fusion
  148.5 1.4 copy.30
  149.9 14.3 all-to-all-done.3
  164.2 2.0 broadcast_in_dim.25
  166.2 6.4 all-to-all-start.7
  173.5 1.8 convert_reduce_fusion.1
  176.5 1.7 fusion.1
  179.5 10.0 collective-permute-done.4
  190.7 10.1 all-to-all-done.7
  202.1 17.5 %all-to-all-start.6 = ((bf16[128,2,1536]{2,1,0:T(2,128)(2,1)}), bf16[128,2,1536]{2,1,0:T(2,128)(2,1)}, u32[]{:S(2)}, u32[]{:S(2)}) async-start(bf16[128,2,1536]{2,1,0:T(2,128)(2,1)} %bitcast.138), calls=%async_computation.6 | async-start | bytes 1572864 | tf_op jit(solution)/shard_map/all_to_all | solution.py:93
  221.0 2.3 reshape.255
  224.4 2.7 collective-permute-start.7
  227.1 15.9 %all-to-all-done.6 = bf16[128,2,1536]{2,1,0:T(2,128)(2,1)} async-done(((bf16[128,2,1536]{2,1,0:T(2,128)(2,1)}), bf16[128,2,1536]{2,1,0:T(2,128)(2,1)}, u32[]{:S(2)}, u32[]{:S(2)}) %all-to-all-start.6) | async-done | bytes 786464 | tf_op jit(solution)/shard_map/all_to_all | solution.py:93
  242.9 3.0 reshape.252
  245.9 1.8 fusion.16
  247.7 3.1 collective-permute-start.5
  251.0 1.8 add.99
  252.8 1.9 collective-permute-start.8
  255.5 3.4 collective-permute-start.6
  259.0 15.3 %all_to_all.54 = bf16[128,1,2]{2,1,0:T(2,128)(2,1)S(1)} all-to-all(bf16[128,1,2]{2,1,0:T(2,128)(2,1)S(1)} %broadcast_in_dim.23), channel_id=1, replica_groups=mesh['dp'=128,'section'=4] {'dp'}, dimensions={0} | all-to-all | bytes 1024 | tf_op jit(solution)/shard_map/all_to_all | solution.py:94
  275.2 2.0 multiply_reduce_fusion
  278.0 5.8 all-to-all-start.9
  283.9 2.2 convolution_convert_fusion.4
  286.1 2.8 reshape.256
  288.9 5.1 all-to-all-done.9
  294.0 7.3 all-to-all-start.8
  302.7 1.7 fusion.27
  309.3 15.6 %all-to-all-done.8 = bf16[128,2,1536]{2,1,0:T(2,128)(2,1)} async-done(((bf16[128,2,1536]{2,1,0:T(2,128)(2,1)}), bf16[128,2,1536]{2,1,0:T(2,128)(2,1)}, u32[]{:S(2)}, u32[]{:S(2)}) %all-to-all-start.8) | async-done | bytes 786464 | tf_op jit(solution)/shard_map/all_to_all | solution.py:124
  324.9 1.8 convert_reduce_fusion
  330.0 1158.5 %all-reduce.2.cloned.1.call-done = f32[6144,8]{0,1:T(8,128)} async-done(((f32[6144,8]{0,1:T(8,128)}), f32[6144,8]{0,1:T(8,128)}) %all-reduce.2.cloned.1.call-update) | async-done | bytes 196624 | tf_op jit(solution)/shard_map/psum | solution.py:140
  1488.5 1.6 copy.48
  (133 shorter events, 40.4 us)
Async XLA Ops:
  7.2 54.1 %copy-start = (bf16[1,1,1536,256]{3,2,1,0:T(8,128)(2,1)S(1)}, bf16[1,1,1536,256]{3,2,1,0:T(8,128)(2,1)}, u32[]{:S(2)}) copy-start(bf16[1,1,1536,256]{3,2,1,0:T(8,128)(2,1)} %param.14) | copy-start | bytes 2359300
  10.7 17.3 %copy-start.12 = (bf16[1,6,6144]{2,1,0:T(8,128)(2,1)S(1)}, bf16[1,6,6144]{2,1,0:T(8,128)(2,1)}, u32[]{:S(2)}) copy-start(bf16[1,6,6144]{2,1,0:T(8,128)(2,1)} %param.9) | copy-start | bytes 221188
  12.7 84.0 %copy-start.21 = (pred[2,6]{1,0:T(4,128)(4,1)}, pred[2,6]{1,0:T(4,128)(4,1)S(1)}, u32[]{:S(2)}) copy-start(pred[2,6]{1,0:T(4,128)(4,1)S(1)} %compare_and_fusion.1) | copy-start | bytes 40
  14.2 37.7 %all-to-all-start.2 = ((bf16[128,2,1536]{2,1,0:T(2,128)(2,1)}), bf16[128,2,1536]{2,1,0:T(2,128)(2,1)S(1)}, u32[]{:S(2)}, u32[]{:S(2)}) async-start(bf16[128,2,1536]{2,1,0:T(2,128)(2,1)} %bitcast.12), calls=%async_computation.2 | async-start | bytes 1572864 | tf_op jit(solution)/shard_map/all_to_all | solution.py:92
  28.0 32.5 %copy-start.4 = (f32[1,6144,8]{1,2,0:T(8,128)S(1)}, f32[1,6144,8]{1,2,0:T(8,128)}, u32[]{:S(2)}) copy-start(f32[1,6144,8]{1,2,0:T(8,128)} %param.13) | copy-start | bytes 589828
  53.1 31.1 %all-to-all-start.1 = ((bf16[128,2,1536]{2,1,0:T(2,128)(2,1)}), bf16[128,2,1536]{2,1,0:T(2,128)(2,1)}, u32[]{:S(2)}, u32[]{:S(2)}) async-start(bf16[128,2,1536]{2,1,0:T(2,128)(2,1)} %bitcast.9), calls=%async_computation.1 | async-start | bytes 1572864 | tf_op jit(solution)/shard_map/all_to_all | solution.py:93
  61.3 25.2 %copy-start.1 = (bf16[1,1,256,1536]{3,2,1,0:T(8,128)(2,1)S(1)}, bf16[1,1,256,1536]{3,2,1,0:T(8,128)(2,1)}, u32[]{:S(2)}) copy-start(bf16[1,1,256,1536]{3,2,1,0:T(8,128)(2,1)} %param.15) | copy-start | bytes 2359300
  62.5 27.8 %collective-permute-start.2 = (f32[256,256]{0,1:T(8,128)}, f32[256,256]{0,1:T(8,128)}, u32[]{:S(2)}, u32[]{:S(2)}) collective-permute-start(f32[256,256]{0,1:T(8,128)} %fusion.14), channel_id=1, source_target_pairs={{0,4},{4,0},{8,12},{12,8},{16,20},{20,16},{24,28},{28,24},{32,36},... | collective-permute-start | bytes 786440 | tf_op jit(solution)/shard_map/ppermute | solution.py:23
  86.9 6.4 collective-permute-start
  90.1 3.2 copy-start.14
  90.2 6.6 copy-start.26
  91.3 32.9 %copy-start.5 = (f32[256,256]{0,1:T(8,128)}, f32[256,256]{0,1:T(8,128)S(1)}, u32[]{:S(2)}) copy-start(f32[256,256]{0,1:T(8,128)S(1)} %add.89) | copy-start | bytes 786436
  91.3 23.8 %collective-permute-start.3 = (f32[256,256]{0,1:T(8,128)S(1)}, f32[256,256]{0,1:T(8,128)S(1)}, u32[]{:S(2)}, u32[]{:S(2)}) collective-permute-start(f32[256,256]{0,1:T(8,128)S(1)} %add.89), channel_id=1, source_target_pairs={{0,8},{8,0},{4,12},{12,4},{16,24},{24,16},{20,28},{28,20},{32,40},... | collective-permute-start | bytes 786440 | tf_op jit(solution)/shard_map/ppermute | solution.py:23
  93.3 21.8 %collective-permute-start.1 = (f32[256,256]{0,1:T(8,128)S(1)}, f32[256,256]{0,1:T(8,128)}, u32[]{:S(2)}, u32[]{:S(2)}) collective-permute-start(f32[256,256]{0,1:T(8,128)S(1)} %add.87), channel_id=1, source_target_pairs={{0,8},{8,0},{4,12},{12,4},{16,24},{24,16},{20,28},{28,20},{32,40},... | collective-permute-start | bytes 786440 | tf_op jit(solution)/shard_map/ppermute | solution.py:23
  97.5 15.8 %all-to-all-start = ((bf16[128,1,2]{2,1,0:T(2,128)(2,1)}), bf16[128,1,2]{2,1,0:T(2,128)(2,1)S(1)}, u32[]{:S(2)}, u32[]{:S(2)}) async-start(bf16[128,1,2]{2,1,0:T(2,128)(2,1)} %broadcast_in_dim.20), calls=%async_computation | async-start | bytes 131072 | tf_op jit(solution)/shard_map/all_to_all | solution.py:94
  115.1 2.7 copy-start.17
  115.1 9.1 copy-start.10
  117.8 16.5 %all-to-all-start.4 = ((bf16[128,1,2]{2,1,0:T(2,128)(2,1)}), bf16[128,1,2]{2,1,0:T(2,128)(2,1)S(1)}, u32[]{:S(2)}, u32[]{:S(2)}) async-start(bf16[128,1,2]{2,1,0:T(2,128)(2,1)} %convert_element_type.182), calls=%async_computation.4 | async-start | bytes 131072 | tf_op jit(solution)/shard_map/all_to_all | solution.py:127
  134.3 29.9 %all-to-all-start.3 = ((bf16[128,2,1536]{2,1,0:T(2,128)(2,1)}), bf16[128,2,1536]{2,1,0:T(2,128)(2,1)S(1)}, u32[]{:S(2)}, u32[]{:S(2)}) async-start(bf16[128,2,1536]{2,1,0:T(2,128)(2,1)} %reshape.246), calls=%async_computation.3 | async-start | bytes 1572864 | tf_op jit(solution)/shard_map/all_to_all | solution.py:124
  144.9 0.6 copy-start.22
  164.2 2.0 copy-start.3
  166.2 34.6 %all-to-all-start.7 = ((bf16[128,2,1536]{2,1,0:T(2,128)(2,1)}), bf16[128,2,1536]{2,1,0:T(2,128)(2,1)S(1)}, u32[]{:S(2)}, u32[]{:S(2)}) async-start(bf16[128,2,1536]{2,1,0:T(2,128)(2,1)} %bitcast.137), calls=%async_computation.7 | async-start | bytes 1572864 | tf_op jit(solution)/shard_map/all_to_all | solution.py:92
  172.6 5.6 copy-start.19
  172.8 16.8 %copy-start.23 = (pred[2,6]{1,0:T(4,128)(4,1)S(1)}, pred[2,6]{1,0:T(4,128)(4,1)}, u32[]{:S(2)}) copy-start(pred[2,6]{1,0:T(4,128)(4,1)} %copy-done.22) | copy-start | bytes 40
  173.5 6.0 copy-start.25
  178.2 11.3 collective-permute-start.4
  200.8 18.8 %copy-start.2 = (bf16[128,2,1536]{2,1,0:T(2,128)(2,1)}, bf16[128,2,1536]{2,1,0:T(2,128)(2,1)S(1)}, u32[]{:S(2)}) copy-start(bf16[128,2,1536]{2,1,0:T(2,128)(2,1)S(1)} %all-to-all-done.7) | copy-start | bytes 2359300
  202.1 40.9 %all-to-all-start.6 = ((bf16[128,2,1536]{2,1,0:T(2,128)(2,1)}), bf16[128,2,1536]{2,1,0:T(2,128)(2,1)}, u32[]{:S(2)}, u32[]{:S(2)}) async-start(bf16[128,2,1536]{2,1,0:T(2,128)(2,1)} %bitcast.138), calls=%async_computation.6 | async-start | bytes 1572864 | tf_op jit(solution)/shard_map/all_to_all | solution.py:93
  224.4 26.6 %collective-permute-start.7 = (f32[256,256]{0,1:T(8,128)}, f32[256,256]{0,1:T(8,128)}, u32[]{:S(2)}, u32[]{:S(2)}) collective-permute-start(f32[256,256]{0,1:T(8,128)} %fusion.11), channel_id=1, source_target_pairs={{0,4},{4,0},{8,12},{12,8},{16,20},{20,16},{24,28},{28,24},{32,36},... | collective-permute-start | bytes 786440 | tf_op jit(solution)/shard_map/ppermute | solution.py:23
  247.7 7.1 collective-permute-start.5
  250.9 23.5 %copy-start.15 = (f32[6,8]{1,0:T(8,128)}, f32[6,8]{1,0:T(8,128)S(1)}, u32[]{:S(2)}) copy-start(f32[6,8]{1,0:T(8,128)S(1)} %broadcast_divide_fusion) | copy-start | bytes 580
  251.0 8.0 copy-start.27
  252.8 22.4 %collective-permute-start.8 = (f32[256,256]{0,1:T(8,128)}, f32[256,256]{0,1:T(8,128)}, u32[]{:S(2)}, u32[]{:S(2)}) collective-permute-start(f32[256,256]{0,1:T(8,128)} %add.99), channel_id=1, source_target_pairs={{0,8},{8,0},{4,12},{12,4},{16,24},{24,16},{20,28},{28,20},{32,40},... | collective-permute-start | bytes 786440 | tf_op jit(solution)/shard_map/ppermute | solution.py:23
  255.5 19.8 %collective-permute-start.6 = (f32[256,256]{0,1:T(8,128)}, f32[256,256]{0,1:T(8,128)}, u32[]{:S(2)}, u32[]{:S(2)}) collective-permute-start(f32[256,256]{0,1:T(8,128)} %add.97), channel_id=1, source_target_pairs={{0,8},{8,0},{4,12},{12,4},{16,24},{24,16},{20,28},{28,20},{32,40},... | collective-permute-start | bytes 786440 | tf_op jit(solution)/shard_map/ppermute | solution.py:23
  278.0 16.0 %all-to-all-start.9 = ((bf16[128,1,2]{2,1,0:T(2,128)(2,1)}), bf16[128,1,2]{2,1,0:T(2,128)(2,1)S(1)}, u32[]{:S(2)}, u32[]{:S(2)}) async-start(bf16[128,1,2]{2,1,0:T(2,128)(2,1)} %convert_element_type.183), calls=%async_computation.9 | async-start | bytes 131072 | tf_op jit(solution)/shard_map/all_to_all | solution.py:127
  294.0 30.9 %all-to-all-start.8 = ((bf16[128,2,1536]{2,1,0:T(2,128)(2,1)}), bf16[128,2,1536]{2,1,0:T(2,128)(2,1)}, u32[]{:S(2)}, u32[]{:S(2)}) async-start(bf16[128,2,1536]{2,1,0:T(2,128)(2,1)} %reshape.256), calls=%async_computation.8 | async-start | bytes 1572864 | tf_op jit(solution)/shard_map/all_to_all | solution.py:124
  301.4 1187.2 %all-reduce.2.cloned.1.call-start = ((), (), s32[]{:S(2)}) async-start(), calls=%async_computation.10 | async-start | bytes 393216 | tf_op jit(solution)/shard_map/psum | solution.py:140
  301.6 2.8 copy-start.6
  301.6 2.8 copy-start.11
  301.6 2.8 copy-start.18
  304.5 1.3 copy-start.9
  305.7 0.9 copy-start.8
  306.6 1.5 copy-start.24
  306.7 1.5 copy-start.28
  306.7 1.6 copy-start.7
  306.7 1.6 copy-start.16
  306.7 1.6 copy-start.20
  308.0 19.0 %copy-start.13 = (bf16[6,6144]{1,0:T(8,128)(2,1)S(1)}, bf16[6,6144]{1,0:T(8,128)(2,1)}, u32[]{:S(2)}) copy-start(bf16[6,6144]{1,0:T(8,128)(2,1)} %param.10) | copy-start | bytes 221188
Sparse Core Ops, SparseCore 0:
  309.4 1179.0 all-reduce.1
where the time goes:
time: 1510 us; the launch traced here: 1500 us
  waiting for transfers between devices  1290 us (85%)
  starting transfers between devices  100 us (7%)
  local copies, waits for them, and re-layouts  33 us (2%)
  matrix products  25.2 us (2%)
  other arithmetic  17.6 us (1%)
  between operations  16.3 us (1%)
  blocking collectives  15.3 us (1%)
    psum x1, waiting for transfers between devices, local(): acc_router = acc_router + lax.psum(router_term, 'dp')  1160 us
    all_to_all x2, waiting for transfers between devices, local(): lax.all_to_all(ysend, 'dp', split_axis=0, concat_axis=0, tiled=True)  34.6 us
    all_to_all x2, waiting for transfers between devices, local(): lax.all_to_all(xsend, 'dp', split_axis=0, concat_axis=0, tiled=True)  33.7 us
  transfers between devices with their start and end apart: 19, of which 11 were waited for; matrix products, arithmetic and copies ran while one was open for 4% of the time, Pallas kernels for 0%

commit v1 on v0

v1 whole, which is shorter than its diff:
```python
import functools

import jax
import jax.numpy as jnp
from jax import lax
from jax.experimental import pallas as pl
from jax.experimental.pallas import tpu as pltpu
from jax.sharding import PartitionSpec as P

STEPS = 2
CAP = 2
EXT = 128


def shifted(array, axis, by):
    devices = lax.axis_size(axis)
    pairs = [(i, i + by) for i in range(devices) if 0 <= i + by < devices]
    return lax.ppermute(array, axis, pairs)


def rounded(value):
    return value.astype(jnp.bfloat16).astype(jnp.float32)


def split_ext(value):
    lanes = lax.broadcasted_iota(jnp.int32, value.shape[:-1] + (EXT,), len(value.shape) - 1)
    high = rounded(value)
    return jnp.where(lanes < EXT // 2, high, value - high)


def step_kernel(first_step, part, hidden, *refs):
    if first_step:
        (pay, w_in, w_out, back, gin, gout, xq, near, rows, pu, ra, sb, rb, dd,
         dx, rx, dz, rz, fin, split, rf, send, recv, own) = refs
        acc_in = acc_out = None
    else:
        (pay, w_in, w_out, acc_in, acc_out, back, gin, gout, xq, near, rows, pu, ra, sb, rb, dd,
         dx, rx, dz, rz, fin, split, rf, send, recv, own) = refs
    wide = part + EXT
    f32 = jnp.float32
    me = lax.axis_index("dp")
    line = me % 8
    base = me - line
    core = me % 2
    odd = (me // 2) % 2
    xpos = (me // 8) % 4
    zpos = me // 32

    def near_dev(r):
        return base + (line + r) % 8

    def z_dev(r):
        return ((zpos + r) % 4) * 32 + xpos * 8 + line

    def x_dev(r):
        return zpos * 32 + ((xpos + r) % 4) * 8 + line

    core_dev = base + (line // 2) * 2 + (1 - core)
    odd_dev = base + (line // 4) * 4 + (1 - odd) * 2 + core

    barrier = pltpu.get_barrier_semaphore()
    peers = [near_dev(r) for r in range(1, 8)]
    peers += [z_dev(r) for r in range(1, 4)] + [x_dev(r) for r in range(1, 4)]
    for peer in peers:
        pl.semaphore_signal(barrier, inc=1, device_id={"dp": peer}, device_id_type=pl.DeviceIdType.MESH)
    pl.semaphore_wait(barrier, len(peers))

    def copy(src, dst, slot, device):
        return pltpu.make_async_remote_copy(
            src_ref=src, dst_ref=dst, send_sem=send.at[slot], recv_sem=recv.at[slot],
            device_id={"dp": device}, device_id_type=pl.DeviceIdType.MESH)

    mine = pltpu.make_async_copy(pay.at[line % 4], near.at[line], own.at[0])
    mine.start()
    sent = []
    for r in range(1, 8):
        c = copy(pay.at[(line + r) % 4], near.at[line], r - 1, near_dev(r))
        c.start()
        sent.append(c)
    mine.wait()
    for r in range(1, 8):
        copy(pay.at[0], near.at[(line + 8 - r) % 8], r - 1, near_dev(r)).wait_recv()
    total = 2 * part + EXT
    chunk = 640
    for at in range(0, total, chunk):
        index = lax.broadcasted_iota(jnp.int32, (16, chunk), 0)
        block = jnp.zeros((16, chunk), f32)
        for s in range(8):
            pair = near[s, :, at:at + chunk].astype(f32)
            for k in range(2):
                block = jnp.where(index == 2 * s + k, pair[k:k + 1], block)
        rows[zpos, xpos, :, at:at + chunk] = block.astype(jnp.bfloat16)
    for r in range(1, 4):
        c = copy(rows.at[zpos, xpos], rows.at[zpos, xpos], 6 + r, z_dev(r))
        c.start()
        sent.append(c)
    for r in range(1, 4):
        copy(rows.at[zpos, xpos], rows.at[(zpos + 4 - r) % 4, xpos], 6 + r, z_dev(r)).wait_recv()
    for r in range(1, 4):
        c = copy(rows.at[:, xpos], rows.at[:, xpos], 9 + r, x_dev(r))
        c.start()
        sent.append(c)
    for r in range(1, 4):
        copy(rows.at[:, xpos], rows.at[:, (xpos + 4 - r) % 4], 9 + r, x_dev(r)).wait_recv()

    def matrix(low, high):
        return rows[:, :, :, low:high].reshape(256, high - low)

    pre = jnp.dot(matrix(0, part), w_in[...], preferred_element_type=f32)
    pu[:, :, 0:hidden] = pre.reshape(4, 64, hidden)
    upper = lax.dot_general(matrix(part, 2 * part), w_out[...], (((1,), (1,)), ((), ())), preferred_element_type=f32)
    pu[:, :, hidden:2 * hidden] = upper.reshape(4, 64, hidden)

    c = copy(pu.at[pl.ds(2 * (1 - core), 2)], ra, 13, core_dev)
    c.start()
    sent.append(c)
    c.wait_recv()
    sb[...] = pu[pl.ds(2 * core, 2)] + ra[...]
    c = copy(sb.at[1 - odd], rb, 14, odd_dev)
    c.start()
    sent.append(c)
    c.wait_recv()
    k = 2 * core + odd
    both = sb[odd] + rb[...]
    pre = both[:, 0:hidden]
    upper = both[:, hidden:2 * hidden]
    gate = rows[k, :, :, 2 * part:2 * part + EXT].reshape(64, EXT).astype(f32)[:, 0:1]
    sig = jax.nn.sigmoid(pre)
    act = pre * sig
    dd[k, :, 0:hidden] = (gate * upper * (sig * (1.0 + pre * (1.0 - sig)))).astype(jnp.bfloat16)
    dd[k, :, hidden:2 * hidden] = (gate * act).astype(jnp.bfloat16)
    sums = jnp.sum(act * upper, axis=1, keepdims=True)
    dd[k, :, 2 * hidden:2 * hidden + EXT] = jnp.broadcast_to(sums, (64, EXT)).astype(jnp.bfloat16)
    c = copy(dd.at[k], dd.at[k], 15, odd_dev)
    c.start()
    sent.append(c)
    copy(dd.at[k], dd.at[2 * core + 1 - odd], 15, odd_dev).wait_recv()
    c = copy(dd.at[pl.ds(2 * core, 2)], dd.at[pl.ds(2 * core, 2)], 16, core_dev)
    c.start()
    sent.append(c)
    copy(dd.at[pl.ds(2 * core, 2)], dd.at[pl.ds(2 * (1 - core), 2)], 16, core_dev).wait_recv()

    dpre = dd[:, :, 0:hidden].reshape(256, hidden)
    scaled = dd[:, :, hidden:2 * hidden].reshape(256, hidden)
    term = lax.dot_general(dpre, w_in[...], (((1,), (1,)), ((), ())), preferred_element_type=f32)
    dx[:, :, :, 0:part] = term.astype(jnp.bfloat16).reshape(4, 4, 16, part)
    sums = dd[:, :, 2 * hidden:2 * hidden + EXT].reshape(256, EXT).astype(f32)
    lanes = lax.broadcasted_iota(jnp.int32, (256, EXT), 1)
    sums = jnp.where(lanes < EXT // 2, sums, 0.0)
    dx[:, :, :, part:wide] = sums.astype(jnp.bfloat16).reshape(4, 4, 16, EXT)
    for r in range(1, 4):
        c = copy(dx.at[:, (xpos + r) % 4], rx.at[r - 1], 16 + r, x_dev(r))
        c.start()
        sent.append(c)
    one = lax.dot_general(matrix(0, part), dpre, (((0,), (0,)), ((), ())), preferred_element_type=f32)
    two = lax.dot_general(scaled, matrix(part, 2 * part), (((0,), (0,)), ((), ())), preferred_element_type=f32)
    if first_step:
        gin[...] = one
        gout[...] = two
    else:
        gin[...] = (acc_in[...] + one).astype(jnp.bfloat16)
        gout[...] = (acc_out[...] + two).astype(jnp.bfloat16)
    xq[...] = matrix(0, part)
    for r in range(1, 4):
        copy(dx.at[:, 0], rx.at[r - 1], 16 + r, x_dev(r)).wait_recv()
    for z in range(4):
        value = dx[z, xpos].astype(f32)
        for r in range(3):
            value = value + rx[r, z].astype(f32)
        dz[z, :, 0:part] = value[:, 0:part].astype(jnp.bfloat16)
        column = value[:, part:part + 1] + value[:, part + EXT // 2:part + EXT // 2 + 1]
        dz[z, :, part:wide] = split_ext(column).astype(jnp.bfloat16)
    for r in range(1, 4):
        c = copy(dz.at[(zpos + r) % 4], rz.at[r - 1], 19 + r, z_dev(r))
        c.start()
        sent.append(c)
    for r in range(1, 4):
        copy(dz.at[0], rz.at[r - 1], 19 + r, z_dev(r)).wait_recv()
    value = dz[zpos].astype(f32)
    for r in range(3):
        value = value + rz[r].astype(f32)
    fin[:, 0:part] = value[:, 0:part]
    column = value[:, part:part + 1] + value[:, part + EXT // 2:part + EXT // 2 + 1]
    fin[:, part:wide] = jnp.broadcast_to(column, (16, EXT))
    for s in range(8):
        split[s] = fin[2 * s:2 * s + 2, :]
    mine = pltpu.make_async_copy(split.at[line], rf.at[line], own.at[1])
    mine.start()
    for r in range(1, 8):
        c = copy(split.at[(line + r) % 8], rf.at[line], 22 + r, near_dev(r))
        c.start()
        sent.append(c)
    mine.wait()
    for r in range(1, 8):
        copy(split.at[0], rf.at[(line + 8 - r) % 8], 22 + r, near_dev(r)).wait_recv()
    back[...] = rf[0:4] + rf[4:8]
    for c in sent:
        c.wait_send()


def run_step(first_step, payload, w_in, w_out, *acc):
    part, hidden = w_in.shape
    wide = part + EXT
    total = 2 * part + EXT
    bf16, f32 = jnp.bfloat16, jnp.float32
    grad = f32 if first_step else bf16
    vmem = pl.BlockSpec(memory_space=pltpu.VMEM)
    copies = 30
    return pl.pallas_call(
        functools.partial(step_kernel, first_step, part, hidden),
        out_shape=(
            jax.ShapeDtypeStruct((4, CAP, wide), f32),
            jax.ShapeDtypeStruct((part, hidden), grad),
            jax.ShapeDtypeStruct((hidden, part), grad),
            jax.ShapeDtypeStruct((256, part), bf16),
        ),
        in_specs=[vmem] * (3 + len(acc)),
        out_specs=(vmem,) * 4,
        scratch_shapes=[
            pltpu.VMEM((8, CAP, total), bf16),
            pltpu.VMEM((4, 4, 16, total), bf16),
            pltpu.VMEM((4, 64, 2 * hidden), f32),
            pltpu.VMEM((2, 64, 2 * hidden), f32),
            pltpu.VMEM((2, 64, 2 * hidden), f32),
            pltpu.VMEM((64, 2 * hidden), f32),
            pltpu.VMEM((4, 64, 2 * hidden + EXT), bf16),
            pltpu.VMEM((4, 4, 16, wide), bf16),
            pltpu.VMEM((3, 4, 16, wide), bf16),
            pltpu.VMEM((4, 16, wide), bf16),
            pltpu.VMEM((3, 16, wide), bf16),
            pltpu.VMEM((16, wide), f32),
            pltpu.VMEM((8, CAP, wide), f32),
            pltpu.VMEM((8, CAP, wide), f32),
            pltpu.SemaphoreType.DMA((copies,)),
            pltpu.SemaphoreType.DMA((copies,)),
            pltpu.SemaphoreType.DMA((2,)),
        ],
        compiler_params=pltpu.CompilerParams(
            collective_id=0 if first_step else 1, has_side_effects=True, vmem_limit_bytes=48 << 20
        ),
    )(payload, w_in, w_out, *acc)


def router_kernel(experts, pay, x0, x1, out, near, every, mine, parts, send, recv, own):
    f32 = jnp.float32
    me = lax.axis_index("dp")
    line = me % 8
    base = me - line
    quarter = me % 4
    xpos = (me // 8) % 4
    zpos = me // 32

    def near_dev(r):
        return base + (line + r) % 8

    def z_dev(r):
        return ((zpos + r) % 4) * 32 + xpos * 8 + line

    def x_dev(r):
        return zpos * 32 + ((xpos + r) % 4) * 8 + line

    def quarter_dev(r):
        return base + (line // 4) * 4 + (quarter + r) % 4

    barrier = pltpu.get_barrier_semaphore()
    peers = [near_dev(r) for r in range(1, 8)]
    peers += [z_dev(r) for r in range(1, 4)] + [x_dev(r) for r in range(1, 4)]
    for peer in peers:
        pl.semaphore_signal(barrier, inc=1, device_id={"dp": peer}, device_id_type=pl.DeviceIdType.MESH)
    pl.semaphore_wait(barrier, len(peers))

    def copy(src, dst, slot, device):
        return pltpu.make_async_remote_copy(
            src_ref=src, dst_ref=dst, send_sem=send.at[slot], recv_sem=recv.at[slot],
            device_id={"dp": device}, device_id_type=pl.DeviceIdType.MESH)

    sent = []
    local_copy = pltpu.make_async_copy(pay, near.at[line], own.at[0])
    local_copy.start()
    for r in range(1, 8):
        c = copy(pay, near.at[line], r - 1, near_dev(r))
        c.start()
        sent.append(c)
    local_copy.wait()
    for r in range(1, 8):
        copy(pay, near.at[(line + 8 - r) % 8], r - 1, near_dev(r)).wait_recv()
    index = lax.broadcasted_iota(jnp.int32, (16, 128), 0)
    for step in range(2):
        block = jnp.zeros((16, 128), f32)
        for s in range(8):
            four = near[s]
            for k in range(2):
                block = jnp.where(index == 2 * s + k, four[2 * step + k:2 * step + k + 1], block)
        every[zpos, xpos, step] = block.astype(jnp.bfloat16)
    for r in range(1, 4):
        c = copy(every.at[zpos, xpos], every.at[zpos, xpos], 6 + r, z_dev(r))
        c.start()
        sent.append(c)
    for r in range(1, 4):
        copy(every.at[zpos, xpos], every.at[(zpos + 4 - r) % 4, xpos], 6 + r, z_dev(r)).wait_recv()
    for r in range(1, 4):
        c = copy(every.at[:, xpos], every.at[:, xpos], 9 + r, x_dev(r))
        c.start()
        sent.append(c)
    for r in range(1, 4):
        copy(every.at[:, xpos], every.at[:, (xpos + 4 - r) % 4], 9 + r, x_dev(r)).wait_recv()
    total = None
    for step, x in enumerate((x0, x1)):
        term = lax.dot_general(every[:, :, step].reshape(256, 128), x[...], (((0,), (0,)), ((), ())),
                               preferred_element_type=f32)
        total = term if total is None else total + term
    mine[...] = total[0:experts] + total[experts:2 * experts] + total[2 * experts:3 * experts]
    local_copy = pltpu.make_async_copy(mine, parts.at[quarter], own.at[1])
    local_copy.start()
    for r in range(1, 4):
        c = copy(mine, parts.at[quarter], 12 + r, quarter_dev(r))
        c.start()
        sent.append(c)
    local_copy.wait()
    for r in range(1, 4):
        copy(mine, parts.at[(quarter + 4 - r) % 4], 12 + r, quarter_dev(r)).wait_recv()
    out[...] = parts[...]
    for c in sent:
        c.wait_send()


def run_router(experts, lanes, x0, x1):
    part = x0.shape[1]
    f32 = jnp.float32
    vmem = pl.BlockSpec(memory_space=pltpu.VMEM)
    return pl.pallas_call(
        functools.partial(router_kernel, experts),
        out_shape=jax.ShapeDtypeStruct((4, experts, part), f32),
        in_specs=[vmem] * 3,
        out_specs=vmem,
        scratch_shapes=[
            pltpu.VMEM((8, 8, 128), f32),
            pltpu.VMEM((4, 4, 2, 16, 128), jnp.bfloat16),
            pltpu.VMEM((experts, part), f32),
            pltpu.VMEM((4, experts, part), f32),
            pltpu.SemaphoreType.DMA((16,)),
            pltpu.SemaphoreType.DMA((16,)),
            pltpu.SemaphoreType.DMA((2,)),
        ],
        compiler_params=pltpu.CompilerParams(
            collective_id=2, has_side_effects=True, vmem_limit_bytes=48 << 20
        ),
    )(lanes, x0, x1)


def dlog_slots(table, dlog):
    return jnp.dot(table, dlog, precision=lax.Precision.HIGHEST)


def local(saved_inputs, carried, head_grad, routing, replica_counts, router, w_in, w_out):
    hi = lax.Precision.HIGHEST
    section_count = lax.axis_size("section")
    section_index = lax.axis_index("section")
    dev_index = lax.axis_index("dp")
    width = head_grad.shape[1]
    part = w_in.shape[2]
    experts = router.shape[2]
    router_w = router[0]
    my_count = replica_counts[dev_index]
    first = (jnp.arange(experts) == 0).astype(jnp.float32)
    slots = jnp.arange(CAP, dtype=jnp.int32)

    def prepare(step):
        xin = saved_inputs[0, step]
        ids = routing[0, step]
        live = step + section_index < my_count
        xf = xin.astype(jnp.float32)
        logits = jnp.dot(xf, router_w, precision=hi)
        expo = jnp.exp(logits)
        prob = expo / jnp.sum(expo, axis=1, keepdims=True)
        routed = ((ids[:, 0] == 0) | (ids[:, 1] == 0)) & live
        slot = jnp.cumsum(routed.astype(jnp.int32), dtype=jnp.int32) - 1
        table = ((slot[None, :] == slots[:, None]) & routed[None, :]).astype(jnp.float32)
        xs = jnp.dot(table.astype(jnp.bfloat16), xin, preferred_element_type=jnp.float32).astype(jnp.bfloat16)
        gate = jnp.dot(table, prob[:, 0], precision=hi).astype(jnp.bfloat16)
        return (xf, prob, table, live, xs, gate)

    def quarters(rows):
        return rows.reshape(CAP, 4, part).transpose(1, 0, 2)

    prepared = [prepare(step) for step in range(STEPS)]
    outputs, logs, inputs = [], [], []
    incoming = carried[0]
    acc = ()
    for step in range(STEPS):
        xf, prob, table, live, xs, gate = prepared[step]
        if step == 1:
            passed = shifted(outputs[0], "section", -1)
            incoming = jnp.where(section_index == section_count - 1, head_grad, passed)
        grad_in_tok = jnp.where(live, incoming, jnp.zeros_like(incoming))
        ys = jnp.dot(table.astype(jnp.bfloat16), grad_in_tok, preferred_element_type=jnp.float32).astype(jnp.bfloat16)
        payload = jnp.concatenate(
            [quarters(xs), quarters(ys), jnp.broadcast_to(gate[None, :, None], (4, CAP, EXT))], axis=2)
        back, *acc, xq = run_step(step == 0, payload, w_in[0, 0], w_out[0, 0], *acc)
        dxs = back[:, :, :part].transpose(1, 0, 2).reshape(CAP, width)
        dgate = back[0, :, part]
        dxe = lax.dot_general(table, dxs, (((0,), (0,)), ((), ())), precision=hi)
        dg_tok = lax.dot_general(table, dgate, (((0,), (0,)), ((), ())), precision=hi)
        dlog = (dg_tok * prob[:, 0])[:, None] * (first[None, :] - prob)
        result = grad_in_tok.astype(jnp.float32) + dxe + jnp.dot(dlog, router_w.T, precision=hi)
        outputs.append(result.astype(jnp.bfloat16))
        logs.append(dlog_slots(table, dlog))
        inputs.append(xq)
    lanes = jnp.concatenate(logs)
    high = rounded(lanes)
    middle = rounded(lanes - high)
    low = lanes - high - middle
    lanes = jnp.concatenate([high, middle, low], axis=1)
    lanes = jnp.pad(lanes, ((0, 8 - lanes.shape[0]), (0, 128 - lanes.shape[1])))
    grad_router = run_router(experts, lanes, *inputs).transpose(0, 2, 1).reshape(width, experts)
    return (jnp.stack(outputs)[:, None], acc[0][None, None], acc[1][None, None], grad_router[None])


def solution(mesh):
    in_specs = (
        P("section", None, "dp", None),
        P("section", "dp", None),
        P("dp", None),
        P("section", None, "dp", None),
        P(),
        P("section", None, None),
        P("section", "dp", None, None),
        P("section", "dp", None, None),
    )
    out_specs = (
        P(None, "section", "dp", None),
        P("section", "dp", None, None),
        P("section", "dp", None, None),
        P("section", None, None),
    )
    return jax.shard_map(local, mesh=mesh, in_specs=in_specs, out_specs=out_specs, check_vma=False)
```

time: 1510 us -> 204 us (0.14)
  waiting for transfers between devices: 1290 us -> 12.3 us
  Pallas kernels: 0 us -> 168 us
  starting transfers between devices: 100 us -> 1.28 us
  local copies, waits for them, and re-layouts: 33 us -> 10.4 us
  matrix products: 25.2 us -> 7.05 us
  other arithmetic: 17.6 us -> 1.73 us
  blocking collectives: 15.3 us -> 0 us
    psum x1 -> x0, waiting for transfers between devices: 1160 us -> none  [local(): acc_router = acc_router + lax.psum(router_term, 'dp')]
    pallas_call x0 -> x3, Pallas kernels: none -> 168 us  [the longest x2 150 us: run_step(): pl.pallas_call(functools.partial(step_kernel, first_step, part, hidden),...]
    all_to_all x9 -> x0, waiting for transfers between devices: 121 us -> none  [the longest x2 34.6 us: local(): lax.all_to_all(ysend, 'dp', split_axis=0, concat_axis=0, tiled=True)]
    all_to_all x9 -> x0, starting transfers between devices: 76.3 us -> none  [the longest x2 24.9 us: local(): lax.all_to_all(ysend, 'dp', split_axis=0, concat_axis=0, tiled=True)]
    ppermute x8 -> x0, starting transfers between devices: 22.5 us -> none  [from_partner(): return lax.ppermute(block, axis, route)]
    all_to_all x1 -> x0, blocking collectives: 15.3 us -> none  [local(): lax.all_to_all(gsend, 'dp', split_axis=0, concat_axis=0, tiled=True)]
  transfers between devices with their start and end apart: 19 -> 1, of which waited for: 11 -> 1; matrix products, arithmetic and copies ran while one was open for 4% -> 1% of each run, Pallas kernels for 0% -> 0%
where the time goes in v1:
time: 204 us; the launch traced here: 203 us
  Pallas kernels  168 us (82%)
  waiting for transfers between devices  12.3 us (6%)
  local copies, waits for them, and re-layouts  10.4 us (5%)
  matrix products  7.05 us (3%)
  between operations  2.22 us (1%)
    pallas_call x2, Pallas kernels, run_step(): pl.pallas_call(functools.partial(step_kernel, first_step, part, hidden),...  150 us
    pallas_call x1, Pallas kernels, run_router(): pl.pallas_call(functools.partial(router_kernel, experts), out_shape=jax.S...  18.7 us
    ppermute x1, waiting for transfers between devices, shifted(): return lax.ppermute(array, axis, pairs)  12.3 us
    unnamed x22, local copies, waits for them, and re-layouts  6.43 us
  transfers between devices with their start and end apart: 1, of which 1 were waited for; matrix products, arithmetic and copies ran while one was open for 1% of the time, Pallas kernels for 0%

profile of v1, /device:TPU:1, one launch (start us, length us, event | category | flops | bytes accessed | tf_op | source)
XLA Modules:
  0.0 203.4 jit_solution(7526657244648519286)
XLA Ops:
  0.6 0.0 copy-start
  0.7 0.8 slice_bitcast_fusion.1
  1.5 1.2 dynamic_slice.3
  3.4 0.2 reduce-window.16
  3.6 1.3 fusion.37
  4.8 1.1 convolution_convert_fusion.2
  5.9 0.2 convolution_convert_fusion.3
  6.1 0.4 fusion.39
  6.5 0.1 broadcast_divide_fusion.1
  6.6 0.1 slice_reduce_fusion.1
  6.7 0.1 fusion.1
  6.9 0.1 broadcast_in_dim.10
  6.9 0.1 pad_maximum_fusion.refs_0_
  7.0 0.0 copy-start.2
  7.0 1.1 copy-done.2
  8.2 75.8 %shard_map.111 = (f32[4,2,1664]{2,1,0:T(2,128)S(1)}, f32[1536,256]{1,0:T(8,128)S(1)}, f32[256,1536]{1,0:T(8,128)S(1)}, bf16[256,1536]{1,0:T(8,128)(2,1)S(1)}) custom-call(bf16[4,2,3200]{2,1,0:T(2,128)(2,1)S(1)} %pad_maximum_fusion.refs_0_, bf16[1536,256]{1,0:T(8,128)(2,1)S(1)} %bitcast.110, bf16[256,1536]{1,0:T(8,128)(2,1)S(1)} %bitcast.112), custom_call_target="tpu_custom_call" | custom-call | tf_op jit(solution)/shard_map/pallas_call | solution.py:209
  83.9 1.1 copy-done.4
  85.1 0.9 copy-done.5
  86.0 0.1 slice_reduce_fusion.3
  86.1 0.1 fusion.3
  86.2 0.3 convolution_add_fusion.1
  86.5 1.0 fusion
  87.5 1.3 collective-permute-start
  88.8 0.2 fusion.13
  89.7 0.2 reduce-window.17
  89.9 0.4 fusion.38
  90.3 0.2 convolution_convert_fusion.1
  90.5 0.1 broadcast_divide_fusion
  90.6 0.1 slice_reduce_fusion
  90.7 0.1 fusion.2
  90.8 12.3 %collective-permute-done = bf16[6,6144]{1,0:T(8,128)(2,1)} collective-permute-done((bf16[6,6144]{1,0:T(8,128)(2,1)}, bf16[6,6144]{1,0:T(8,128)(2,1)}, u32[]{:S(2)}, u32[]{:S(2)}) %collective-permute-start) | collective-permute-done | bytes 73760 | tf_op jit(solution)/shard_map/ppermute | solution.py:18
  103.1 1.0 convolution_convert_fusion
  104.2 0.1 broadcast_in_dim.11
  104.3 0.1 pad_maximum_fusion.1.refs_0_
  104.3 0.0 copy-start.6
  104.3 74.0 %shard_map.112 = (f32[4,2,1664]{2,1,0:T(2,128)S(1)}, bf16[1536,256]{1,0:T(8,128)(2,1)S(1)}, bf16[256,1536]{1,0:T(8,128)(2,1)S(1)}, bf16[256,1536]{1,0:T(8,128)(2,1)S(1)}) custom-call(bf16[4,2,3200]{2,1,0:T(2,128)(2,1)S(1)} %pad_maximum_fusion.1.refs_0_, bf16[1536,256]{1,0:T(8,128)(2,1)S(1)} %bitcast.111, bf16[256,1536]{1,0:T(8,128)(2,1)S(1)} %bitcast.113, ...), custom_call_target="tpu_custom_call" | custom-call | tf_op jit(solution)/shard_map/pallas_call | solution.py:209
  178.4 0.1 slice_reduce_fusion.2
  178.5 0.1 fusion.4
  178.6 0.2 fusion.14
  178.8 0.1 select_maximum_fusion.pay
  178.9 18.7 %shard_map.113 = f32[4,8,1536]{2,1,0:T(8,128)S(1)} custom-call(f32[8,128]{1,0:T(8,128)S(1)} %select_maximum_fusion.pay, bf16[256,1536]{1,0:T(8,128)(2,1)S(1)} %copy-done.6, bf16[256,1536]{1,0:T(8,128)(2,1)S(1)} %get-tuple-element.19.x1), custom_call_target="tpu_custom_call" | custom-call | tf_op jit(solution)/shard_map/pallas_call | solution.py:331
  197.6 0.3 fusion.40
  197.9 1.3 fusion.10
  199.2 0.9 maximum_bitcast_fusion
  200.1 0.8 copy.15
  201.0 0.9 copy.31
  201.8 0.9 copy.32
  202.7 0.7 copy.33
  (23 shorter events, 0.1 us)
Async XLA Ops:
  0.6 5.4 %copy-start = (f32[1,6144,8]{1,2,0:T(8,128)S(1)}, f32[1,6144,8]{1,2,0:T(8,128)}, u32[]{:S(2)}) copy-start(f32[1,6144,8]{1,2,0:T(8,128)} %param.13) | copy-start | bytes 589828
  0.6 6.4 %copy-start.1 = (bf16[1,1,1536,256]{3,2,1,0:T(8,128)(2,1)S(1)}, bf16[1,1,1536,256]{3,2,1,0:T(8,128)(2,1)}, u32[]{:S(2)}) copy-start(bf16[1,1,1536,256]{3,2,1,0:T(8,128)(2,1)} %param.14) | copy-start | bytes 2359300
  3.5 82.6 %copy-start.7 = (bf16[1,6,6144]{2,1,0:T(8,128)(2,1)S(1)}, bf16[1,6,6144]{2,1,0:T(8,128)(2,1)}, u32[]{:S(2)}) copy-start(bf16[1,6,6144]{2,1,0:T(8,128)(2,1)} %param.9) | copy-start | bytes 221188
  7.0 1.1 copy-start.2
  8.2 96.2 %copy-start.3 = (bf16[1,1,256,1536]{3,2,1,0:T(8,128)(2,1)S(1)}, bf16[1,1,256,1536]{3,2,1,0:T(8,128)(2,1)}, u32[]{:S(2)}) copy-start(bf16[1,1,256,1536]{3,2,1,0:T(8,128)(2,1)} %param.15) | copy-start | bytes 2359300
  83.9 1.2 copy-start.4
  85.1 0.9 copy-start.5
  87.5 15.6 %collective-permute-start = (bf16[6,6144]{1,0:T(8,128)(2,1)}, bf16[6,6144]{1,0:T(8,128)(2,1)}, u32[]{:S(2)}, u32[]{:S(2)}) collective-permute-start(bf16[6,6144]{1,0:T(8,128)(2,1)} %fusion), channel_id=1, source_target_pairs={{1,0},{2,1},{3,2},{5,4},{6,5},{7,6},{9,8},{10,9},{11,10},{13,12},{... | collective-permute-start | bytes 221192 | tf_op jit(solution)/shard_map/ppermute | solution.py:18
  104.3 74.6 %copy-start.6 = (bf16[256,1536]{1,0:T(8,128)(2,1)S(1)}, bf16[256,1536]{1,0:T(8,128)(2,1)}, u32[]{:S(2)}) copy-start(bf16[256,1536]{1,0:T(8,128)(2,1)} %copy-done.5) | copy-start | bytes 2359300
  178.3 19.6 %copy-start.8 = (bf16[6,6144]{1,0:T(8,128)(2,1)S(1)}, bf16[6,6144]{1,0:T(8,128)(2,1)}, u32[]{:S(2)}) copy-start(bf16[6,6144]{1,0:T(8,128)(2,1)} %param.10) | copy-start | bytes 221188

commit v2 on v0

v2 whole, which is shorter than its diff:
```python
import functools

import jax
import jax.numpy as jnp
from jax import lax
from jax.experimental import pallas as pl
from jax.experimental.pallas import tpu as pltpu
from jax.sharding import PartitionSpec as P

STEPS = 2
CAP = 2
EXT = 128


def shifted(array, axis, by):
    devices = lax.axis_size(axis)
    pairs = [(i, i + by) for i in range(devices) if 0 <= i + by < devices]
    return lax.ppermute(array, axis, pairs)


def rounded(value):
    return value.astype(jnp.bfloat16).astype(jnp.float32)


def split_ext(value):
    lanes = lax.broadcasted_iota(jnp.int32, value.shape[:-1] + (EXT,), len(value.shape) - 1)
    high = rounded(value)
    return jnp.where(lanes < EXT // 2, high, value - high)


def step_kernel(first_step, part, hidden, experts, names, *refs):
    ref = dict(zip(names, refs))
    pay_y, w_in, w_out = ref["pay_y"], ref["w_in"], ref["w_out"]
    send, recv, own = ref["send"], ref["recv"], ref["own"]
    wide = part + EXT
    f32, bf16 = jnp.float32, jnp.bfloat16
    me = lax.axis_index("dp")
    line = me % 8
    base = me - line
    core = me % 2
    odd = (me // 2) % 2
    half = line // 4
    quarter = me % 4
    xpos = (me // 8) % 4
    zpos = me // 32
    ahead, behind, across = (xpos + 1) % 4, (xpos + 3) % 4, (xpos + 2) % 4

    def near_dev(r):
        return base + (line + r) % 8

    def z_dev(r):
        return ((zpos + r) % 4) * 32 + xpos * 8 + line

    def x_dev(r):
        return zpos * 32 + ((xpos + r) % 4) * 8 + line

    core_dev = base + (line // 2) * 2 + (1 - core)
    odd_dev = base + half * 4 + (1 - odd) * 2 + core
    half_dev = base + (line + 4) % 8

    barrier = pltpu.get_barrier_semaphore()
    peers = [near_dev(r) for r in range(1, 8)]
    peers += [z_dev(r) for r in range(1, 4)] + [x_dev(r) for r in range(1, 4)]
    for peer in peers:
        pl.semaphore_signal(barrier, inc=1, device_id={"dp": peer}, device_id_type=pl.DeviceIdType.MESH)
    pl.semaphore_wait(barrier, len(peers))

    def copy(src, dst, slot, device):
        return pltpu.make_async_remote_copy(
            src_ref=src, dst_ref=dst, send_sem=send.at[slot], recv_sem=recv.at[slot],
            device_id={"dp": device}, device_id_type=pl.DeviceIdType.MESH)

    sent, taken, kept = [], [0], [0]

    def slots(count):
        taken[0] += count
        return list(range(taken[0] - count, taken[0]))

    def go(src, dst, slot, device):
        c = copy(src, dst, slot, device)
        c.start()
        sent.append(c)

    def keep(src, dst):
        c = pltpu.make_async_copy(src, dst, own.at[kept[0]])
        kept[0] += 1
        c.start()
        return c

    class Gather:
        def __init__(self, pay, near, rows, columns):
            self.pay, self.near, self.rows, self.columns = pay, near, rows, columns
            self.n, self.z, self.x = slots(7), slots(3), slots(6)

        def near_start(self):
            self.mine = keep(self.pay.at[quarter], self.near.at[line])
            for r in range(1, 8):
                go(self.pay.at[(line + r) % 4], self.near.at[line], self.n[r - 1], near_dev(r))

        def near_wait(self):
            self.mine.wait()
            for r in range(1, 8):
                copy(self.pay.at[0], self.near.at[(line + 8 - r) % 8], self.n[r - 1], near_dev(r)).wait_recv()
            for at in range(0, self.columns, 512):
                size = min(512, self.columns - at)
                index = lax.broadcasted_iota(jnp.int32, (16, size), 0)
                block = jnp.zeros((16, size), f32)
                for s in range(8):
                    pair = self.near[s, :, at:at + size].astype(f32)
                    for k in range(2):
                        block = jnp.where(index == 2 * s + k, pair[k:k + 1], block)
                self.rows[zpos, xpos, :, at:at + size] = block.astype(bf16)

        def z_start(self):
            for r in range(1, 4):
                go(self.rows.at[zpos, xpos], self.rows.at[zpos, xpos], self.z[r - 1], z_dev(r))

        def z_wait(self):
            for r in range(1, 4):
                copy(self.rows.at[zpos, xpos], self.rows.at[(zpos + 4 - r) % 4, xpos], self.z[r - 1], z_dev(r)).wait_recv()

        def piece(self, top, x):
            return self.rows.at[pl.ds(2 * top, 2), x]

        def x_start(self):
            go(self.piece(0, xpos), self.piece(0, xpos), self.x[0], x_dev(1))
            go(self.piece(1, xpos), self.piece(1, xpos), self.x[1], x_dev(3))
            go(self.piece(1, xpos), self.piece(1, xpos), self.x[2], x_dev(1))
            go(self.piece(0, xpos), self.piece(0, xpos), self.x[3], x_dev(3))

        def x_pass(self):
            copy(self.piece(0, xpos), self.piece(0, behind), self.x[0], x_dev(1)).wait_recv()
            go(self.piece(0, behind), self.piece(0, behind), self.x[4], x_dev(1))
            copy(self.piece(1, xpos), self.piece(1, ahead), self.x[1], x_dev(3)).wait_recv()
            go(self.piece(1, ahead), self.piece(1, ahead), self.x[5], x_dev(3))

        def x_wait(self):
            copy(self.piece(1, xpos), self.piece(1, behind), self.x[2], x_dev(1)).wait_recv()
            copy(self.piece(0, xpos), self.piece(0, ahead), self.x[3], x_dev(3)).wait_recv()
            copy(self.piece(0, xpos), self.piece(0, across), self.x[4], x_dev(1)).wait_recv()
            copy(self.piece(1, xpos), self.piece(1, across), self.x[5], x_dev(3)).wait_recv()

    ys = ref["yr"]
    gy = Gather(pay_y, ref["ny"], ys, part)
    if first_step:
        xs = ref["xr"]
        gx = Gather(ref["pay_x"], ref["nx"], xs, wide)
        later = Gather(ref["pay_l"], ref["nl"], ref["lr"], wide)
        now = (gx, gy)
    else:
        xs = ref["xr_in"]
        now = (gy,)
    for g in now:
        g.near_start()
    if first_step:
        later.near_start()
    for g in now:
        g.near_wait()
        g.z_start()
    if first_step:
        later.near_wait()
    for g in now:
        g.z_wait()
        g.x_start()
    if first_step:
        later.z_start()
    for g in now:
        g.x_pass()
    for g in now:
        g.x_wait()
    if first_step:
        later.z_wait()
        later.x_start()

    xmat = xs[:, :, :, 0:part].reshape(256, part)
    pu, ra, sb, rb, dd = ref["pu"], ref["ra"], ref["sb"], ref["rb"], ref["dd"]
    pre = jnp.dot(xmat, w_in[...], preferred_element_type=f32)
    pu[:, :, 0:hidden] = pre.reshape(4, 64, hidden)
    upper = lax.dot_general(ys[...].reshape(256, part), w_out[...], (((1,), (1,)), ((), ())), preferred_element_type=f32)
    pu[:, :, hidden:2 * hidden] = upper.reshape(4, 64, hidden)

    s1, s2, s3, s4 = slots(4)
    go(pu.at[pl.ds(2 * (1 - core), 2)], ra, s1, core_dev)
    copy(pu.at[pl.ds(2 * (1 - core), 2)], ra, s1, core_dev).wait_recv()
    sb[...] = pu[pl.ds(2 * core, 2)] + ra[...]
    go(sb.at[1 - odd], rb, s2, odd_dev)
    if first_step:
        later.x_pass()
    copy(sb.at[1 - odd], rb, s2, odd_dev).wait_recv()
    k = 2 * core + odd
    both = sb[odd] + rb[...]
    pre = both[:, 0:hidden]
    upper = both[:, hidden:2 * hidden]
    gate = xs[k, :, :, part:wide].reshape(64, EXT).astype(f32)[:, 0:1]
    sig = jax.nn.sigmoid(pre)
    act = pre * sig
    dd[k, :, 0:hidden] = (gate * upper * (sig * (1.0 + pre * (1.0 - sig)))).astype(bf16)
    dd[k, :, hidden:2 * hidden] = (gate * act).astype(bf16)
    sums = jnp.sum(act * upper, axis=1, keepdims=True)
    dd[k, :, 2 * hidden:2 * hidden + EXT] = jnp.broadcast_to(sums, (64, EXT)).astype(bf16)
    go(dd.at[k], dd.at[k], s3, odd_dev)
    copy(dd.at[k], dd.at[2 * core + 1 - odd], s3, odd_dev).wait_recv()
    go(dd.at[pl.ds(2 * core, 2)], dd.at[pl.ds(2 * core, 2)], s4, core_dev)
    copy(dd.at[pl.ds(2 * core, 2)], dd.at[pl.ds(2 * (1 - core), 2)], s4, core_dev).wait_recv()

    ax, az, ah = ref["ax"], ref["az"], ref["ah"]
    sums = dd[:, :, 2 * hidden:2 * hidden + EXT].reshape(256, EXT)
    pick = (lax.broadcasted_iota(jnp.int32, (16, EXT), 1) == 0).astype(f32).astype(bf16)
    ax[xpos] = lax.dot_general(pick, sums, (((1,), (1,)), ((), ())), preferred_element_type=f32)[0:8]
    sx, sz = slots(3), slots(3)
    sh, = slots(1)
    for r in range(1, 4):
        go(ax.at[xpos], ax.at[xpos], sx[r - 1], x_dev(r))

    dx, rx, ry, dz, rz = ref["dx"], ref["rx"], ref["ry"], ref["dz"], ref["rz"]
    dpre = dd[:, :, 0:hidden].reshape(256, hidden)
    scaled = dd[:, :, hidden:2 * hidden].reshape(256, hidden)
    term = lax.dot_general(dpre, w_in[...], (((1,), (1,)), ((), ())), preferred_element_type=f32)
    dx[:, :, :, 0:part] = term.astype(bf16).reshape(4, 4, 16, part)
    lanes = lax.broadcasted_iota(jnp.int32, (256, EXT), 1)
    sums = jnp.where(lanes < EXT // 2, sums.astype(f32), 0.0)
    dx[:, :, :, part:wide] = sums.astype(bf16).reshape(4, 4, 16, EXT)

    def piece(top, x):
        return dx.at[pl.ds(2 * top, 2), x]

    if first_step:
        later.x_wait()
    b = slots(6)
    go(piece(0, across), ry.at[0], b[0], x_dev(1))
    go(piece(1, across), ry.at[1], b[1], x_dev(3))
    go(piece(1, ahead), rx.at[0, pl.ds(2, 2)], b[2], x_dev(1))
    go(piece(0, behind), rx.at[1, pl.ds(0, 2)], b[3], x_dev(3))
    for r in range(1, 4):
        copy(ax.at[xpos], ax.at[(xpos + 4 - r) % 4], sx[r - 1], x_dev(r)).wait_recv()
    az[zpos] = ax[0] + ax[1] + ax[2] + ax[3]
    for r in range(1, 4):
        go(az.at[zpos], az.at[zpos], sz[r - 1], z_dev(r))

    def joined(first, second):
        value = first.astype(f32) + second.astype(f32)
        column = value[..., part:part + 1] + value[..., part + EXT // 2:part + EXT // 2 + 1]
        return value[..., 0:part].astype(bf16), split_ext(column).astype(bf16)

    def pass_on(top, x, slot, came, device):
        copy(piece(top, x), ry.at[came], slot, device).wait_recv()
        for z in range(2):
            main, ext = joined(dx[2 * top + z, x], ry[came, z])
            dx[2 * top + z, x, :, 0:part] = main
            dx[2 * top + z, x, :, part:wide] = ext

    pass_on(0, ahead, b[0], 0, x_dev(1))
    go(piece(0, ahead), rx.at[0, pl.ds(0, 2)], b[4], x_dev(1))
    pass_on(1, behind, b[1], 1, x_dev(3))
    go(piece(1, behind), rx.at[1, pl.ds(2, 2)], b[5], x_dev(3))
    one = lax.dot_general(xmat, dpre, (((0,), (0,)), ((), ())), preferred_element_type=f32)
    two = lax.dot_general(scaled, ys[...].reshape(256, part), (((0,), (0,)), ((), ())), preferred_element_type=f32)
    gin, gout = ref["gin"], ref["gout"]
    if first_step:
        gin[...] = one
        gout[...] = two
        ref["xr_out"][...] = ref["lr"][...]
    else:
        gin[...] = (ref["acc_in"][...] + one).astype(bf16)
        gout[...] = (ref["acc_out"][...] + two).astype(bf16)
    for r in range(1, 4):
        copy(az.at[zpos], az.at[(zpos + 4 - r) % 4], sz[r - 1], z_dev(r)).wait_recv()
    ah[half] = az[0] + az[1] + az[2] + az[3]
    go(ah.at[half], ah.at[half], sh, half_dev)
    copy(piece(1, xpos), rx.at[0, pl.ds(2, 2)], b[2], x_dev(1)).wait_recv()
    copy(piece(0, xpos), rx.at[1, pl.ds(0, 2)], b[3], x_dev(3)).wait_recv()
    copy(piece(0, xpos), rx.at[0, pl.ds(0, 2)], b[4], x_dev(1)).wait_recv()
    copy(piece(1, xpos), rx.at[1, pl.ds(2, 2)], b[5], x_dev(3)).wait_recv()
    for z in range(4):
        value = dx[z, xpos].astype(f32) + rx[0, z].astype(f32) + rx[1, z].astype(f32)
        dz[z, :, 0:part] = value[:, 0:part].astype(bf16)
        column = value[:, part:part + 1] + value[:, part + EXT // 2:part + EXT // 2 + 1]
        dz[z, :, part:wide] = split_ext(column).astype(bf16)
    e = slots(3)
    for r in range(1, 4):
        go(dz.at[(zpos + r) % 4], rz.at[r - 1], e[r - 1], z_dev(r))
    copy(ah.at[half], ah.at[1 - half], sh, half_dev).wait_recv()
    dgate = (ah[0] + ah[1])[0:1]
    ext = jnp.transpose(xs[:, :, :, part:wide].reshape(256, EXT).astype(f32))
    slope = ext[8:16] + ext[16:24] + ext[24:32]
    dlog = slope * dgate
    high = rounded(dlog)
    middle = rounded(dlog - high)
    split = jnp.concatenate([high, middle, dlog - high - middle, jnp.zeros_like(high)], axis=0).astype(bf16)
    router = jnp.dot(split, xmat, preferred_element_type=f32)
    router = router[0:8] + router[8:16] + router[16:24]
    if first_step:
        ref["gr"][...] = router
    else:
        mine, parts = ref["mine"], ref["parts"]
        mine[...] = ref["gr_in"][...] + router
        held = keep(mine, parts.at[quarter])
        qs = slots(3)
        for r in range(1, 4):
            go(mine, parts.at[quarter], qs[r - 1], base + half * 4 + (quarter + r) % 4)
    for r in range(1, 4):
        copy(dz.at[0], rz.at[r - 1], e[r - 1], z_dev(r)).wait_recv()
    fin, split, rf = ref["fin"], ref["split"], ref["rf"]
    value = dz[zpos].astype(f32)
    for r in range(3):
        value = value + rz[r].astype(f32)
    fin[:, 0:part] = value[:, 0:part]
    column = value[:, part:part + 1] + value[:, part + EXT // 2:part + EXT // 2 + 1]
    fin[:, part:wide] = jnp.broadcast_to(column, (16, EXT))
    for s in range(8):
        split[s] = fin[2 * s:2 * s + 2, :]
    stay = keep(split.at[line], rf.at[line])
    n = slots(7)
    for r in range(1, 8):
        go(split.at[(line + r) % 8], rf.at[line], n[r - 1], near_dev(r))
    stay.wait()
    for r in range(1, 8):
        copy(split.at[0], rf.at[(line + 8 - r) % 8], n[r - 1], near_dev(r)).wait_recv()
    ref["back"][...] = rf[0:4] + rf[4:8]
    if not first_step:
        held.wait()
        for r in range(1, 4):
            copy(mine, parts.at[(quarter + 4 - r) % 4], qs[r - 1], core_dev).wait_recv()
        ref["gr"][...] = parts[...]
    for c in sent:
        c.wait_send()


def run_step(first_step, experts, ins):
    part, hidden = ins["w_in"].shape
    wide = part + EXT
    bf16, f32 = jnp.bfloat16, jnp.float32
    grad = f32 if first_step else bf16
    outs = {
        "back": ((4, CAP, wide), f32),
        "gin": ((part, hidden), grad),
        "gout": ((hidden, part), grad),
        "gr": ((experts, part) if first_step else (4, experts, part), f32),
    }
    scratch = {
        "ny": ((8, CAP, part), bf16),
        "yr": ((4, 4, 16, part), bf16),
        "pu": ((4, 64, 2 * hidden), f32),
        "ra": ((2, 64, 2 * hidden), f32),
        "sb": ((2, 64, 2 * hidden), f32),
        "rb": ((64, 2 * hidden), f32),
        "dd": ((4, 64, 2 * hidden + EXT), bf16),
        "dx": ((4, 4, 16, wide), bf16),
        "rx": ((2, 4, 16, wide), bf16),
        "ry": ((2, 2, 16, wide), bf16),
        "dz": ((4, 16, wide), bf16),
        "rz": ((3, 16, wide), bf16),
        "ax": ((4, 8, 256), f32),
        "az": ((4, 8, 256), f32),
        "ah": ((2, 8, 256), f32),
        "fin": ((16, wide), f32),
        "split": ((8, CAP, wide), f32),
        "rf": ((8, CAP, wide), f32),
    }
    if first_step:
        outs["xr_out"] = ((4, 4, 16, wide), bf16)
        scratch["nx"] = scratch["nl"] = ((8, CAP, wide), bf16)
        scratch["xr"] = scratch["lr"] = ((4, 4, 16, wide), bf16)
    else:
        scratch["mine"] = ((experts, part), f32)
        scratch["parts"] = ((4, experts, part), f32)
    names = list(ins) + list(outs) + list(scratch) + ["send", "recv", "own"]
    vmem = pl.BlockSpec(memory_space=pltpu.VMEM)
    copies = 80
    got = pl.pallas_call(
        functools.partial(step_kernel, first_step, part, hidden, experts, names),
        out_shape=[jax.ShapeDtypeStruct(*leaf) for leaf in outs.values()],
        in_specs=[vmem] * len(ins),
        out_specs=[vmem] * len(outs),
        scratch_shapes=[pltpu.VMEM(*leaf) for leaf in scratch.values()]
        + [pltpu.SemaphoreType.DMA((copies,)), pltpu.SemaphoreType.DMA((copies,)), pltpu.SemaphoreType.DMA((8,))],
        compiler_params=pltpu.CompilerParams(
            collective_id=0 if first_step else 1, has_side_effects=True, vmem_limit_bytes=48 << 20
        ),
    )(*ins.values())
    return dict(zip(outs, got))


def local(saved_inputs, carried, head_grad, routing, replica_counts, router, w_in, w_out):
    hi = lax.Precision.HIGHEST
    section_count = lax.axis_size("section")
    section_index = lax.axis_index("section")
    dev_index = lax.axis_index("dp")
    width = head_grad.shape[1]
    part = w_in.shape[2]
    experts = router.shape[2]
    router_w = router[0]
    my_count = replica_counts[dev_index]
    first = (jnp.arange(experts) == 0).astype(jnp.float32)
    slots = jnp.arange(CAP, dtype=jnp.int32)

    def quarters(rows):
        return rows.reshape(CAP, 4, part).transpose(1, 0, 2)

    def prepare(step):
        xin = saved_inputs[0, step]
        ids = routing[0, step]
        live = step + section_index < my_count
        xf = xin.astype(jnp.float32)
        logits = jnp.dot(xf, router_w, precision=hi)
        expo = jnp.exp(logits)
        prob = expo / jnp.sum(expo, axis=1, keepdims=True)
        routed = ((ids[:, 0] == 0) | (ids[:, 1] == 0)) & live
        slot = jnp.cumsum(routed.astype(jnp.int32), dtype=jnp.int32) - 1
        table = ((slot[None, :] == slots[:, None]) & routed[None, :]).astype(jnp.float32)
        xs = jnp.dot(table.astype(jnp.bfloat16), xin, preferred_element_type=jnp.float32).astype(jnp.bfloat16)
        gate = jnp.dot(table, prob[:, 0], precision=hi).astype(jnp.bfloat16)
        slope = jnp.dot(table, prob[:, :1] * (first[None, :] - prob), precision=hi)
        high = rounded(slope)
        middle = rounded(slope - high)
        low = rounded(slope - high - middle)
        ext = jnp.concatenate(
            [jnp.broadcast_to(gate.astype(jnp.float32)[:, None], (CAP, 8)), high, middle, low], axis=1)
        ext = jnp.pad(ext, ((0, 0), (0, EXT - ext.shape[1]))).astype(jnp.bfloat16)
        payload = jnp.concatenate([quarters(xs), jnp.broadcast_to(ext[None], (4, CAP, EXT))], axis=2)
        return (prob, table, live, payload)

    prepared = [prepare(step) for step in range(STEPS)]
    outputs = []
    incoming = carried[0]
    weights = {"w_in": w_in[0, 0], "w_out": w_out[0, 0]}
    for step in range(STEPS):
        prob, table, live, payload = prepared[step]
        if step == 1:
            passed = shifted(outputs[0], "section", -1)
            incoming = jnp.where(section_index == section_count - 1, head_grad, passed)
        grad_in_tok = jnp.where(live, incoming, jnp.zeros_like(incoming))
        ys = jnp.dot(table.astype(jnp.bfloat16), grad_in_tok, preferred_element_type=jnp.float32).astype(jnp.bfloat16)
        ins = {"pay_y": quarters(ys), **weights}
        if step == 0:
            ins.update(pay_x=payload, pay_l=prepared[1][3])
        else:
            ins.update(xr_in=got["xr_out"], acc_in=got["gin"], acc_out=got["gout"], gr_in=got["gr"])
        got = run_step(step == 0, experts, ins)
        back = got["back"]
        dxs = back[:, :, :part].transpose(1, 0, 2).reshape(CAP, width)
        dgate = back[0, :, part]
        dxe = lax.dot_general(table, dxs, (((0,), (0,)), ((), ())), precision=hi)
        dg_tok = lax.dot_general(table, dgate, (((0,), (0,)), ((), ())), precision=hi)
        dlog = (dg_tok * prob[:, 0])[:, None] * (first[None, :] - prob)
        result = grad_in_tok.astype(jnp.float32) + dxe + jnp.dot(dlog, router_w.T, precision=hi)
        outputs.append(result.astype(jnp.bfloat16))
    grad_router = got["gr"].transpose(0, 2, 1).reshape(width, experts)
    return (jnp.stack(outputs)[:, None], got["gin"][None, None], got["gout"][None, None], grad_router[None])


def solution(mesh):
    in_specs = (
        P("section", None, "dp", None),
        P("section", "dp", None),
        P("dp", None),
        P("section", None, "dp", None),
        P(),
        P("section", None, None),
        P("section", "dp", None, None),
        P("section", "dp", None, None),
    )
    out_specs = (
        P(None, "section", "dp", None),
        P("section", "dp", None, None),
        P("section", "dp", None, None),
        P("section", None, None),
    )
    return jax.shard_map(local, mesh=mesh, in_specs=in_specs, out_specs=out_specs, check_vma=False)
```

time: 1510 us -> 159 us (0.11)
  waiting for transfers between devices: 1290 us -> 14.9 us
  Pallas kernels: 0 us -> 124 us
  starting transfers between devices: 100 us -> 1.29 us
  local copies, waits for them, and re-layouts: 33 us -> 10.4 us
  matrix products: 25.2 us -> 5.62 us
  other arithmetic: 17.6 us -> 0.8 us
  blocking collectives: 15.3 us -> 0 us
    psum x1 -> x0, waiting for transfers between devices: 1160 us -> none  [local(): acc_router = acc_router + lax.psum(router_term, 'dp')]
    pallas_call x0 -> x2, Pallas kernels: none -> 124 us  [run_step(): pl.pallas_call(functools.partial(step_kernel, first_step, part, hidden, e...]
    all_to_all x9 -> x0, waiting for transfers between devices: 121 us -> none  [the longest x2 34.6 us: local(): lax.all_to_all(ysend, 'dp', split_axis=0, concat_axis=0, tiled=True)]
    all_to_all x9 -> x0, starting transfers between devices: 76.3 us -> none  [the longest x2 24.9 us: local(): lax.all_to_all(ysend, 'dp', split_axis=0, concat_axis=0, tiled=True)]
    ppermute x8 -> x0, starting transfers between devices: 22.5 us -> none  [from_partner(): return lax.ppermute(block, axis, route)]
    all_to_all x1 -> x0, blocking collectives: 15.3 us -> none  [local(): lax.all_to_all(gsend, 'dp', split_axis=0, concat_axis=0, tiled=True)]
  transfers between devices with their start and end apart: 19 -> 1, of which waited for: 11 -> 1; matrix products, arithmetic and copies ran while one was open for 4% -> 0% of each run, Pallas kernels for 0% -> 0%
where the time goes in v2:
time: 159 us
  Pallas kernels  124 us (78%)
  waiting for transfers between devices  14.9 us (9%)
  local copies, waits for them, and re-layouts  10.4 us (7%)
  matrix products  5.62 us (4%)
  between operations  2.18 us (1%)
    pallas_call x2, Pallas kernels, run_step(): pl.pallas_call(functools.partial(step_kernel, first_step, part, hidden, e...  124 us
    ppermute x1, waiting for transfers between devices, shifted(): return lax.ppermute(array, axis, pairs)  14.9 us
    unnamed x20, local copies, waits for them, and re-layouts  6.49 us
  transfers between devices with their start and end apart: 1, of which 1 were waited for; matrix products, arithmetic and copies ran while one was open for 0% of the time, Pallas kernels for 0%

profile of v2, /device:TPU:1, one launch (start us, length us, event | category | flops | bytes accessed | tf_op | source)
XLA Modules:
  0.0 158.9 jit_solution(14345773528350136562)
XLA Ops:
  0.6 0.0 copy-start
  0.6 0.0 copy-start.6
  0.7 0.0 copy-start.2
  0.7 1.4 dynamic_slice.3
  3.4 0.7 slice_bitcast_fusion.1
  4.1 0.2 reduce-window.16
  4.3 0.2 reduce-window.17
  4.5 1.2 fusion.59
  5.7 0.0 copy-done
  5.7 0.5 fusion.63
  6.2 0.2 convolution_convert_fusion.1
  6.4 0.1 broadcast_divide_fusion
  6.4 0.1 slice_reduce_fusion
  6.6 0.1 fusion.2
  6.7 0.2 fusion.60
  6.9 0.5 fusion.62
  7.4 0.2 convolution_convert_fusion.2
  7.6 0.1 broadcast_divide_fusion.1
  7.6 0.1 slice_reduce_fusion.1
  7.7 0.1 fusion.1
  7.9 0.2 fusion.61
  8.1 0.2 convolution_convert_fusion.3
  8.2 0.1 broadcast_in_dim.16
  8.3 0.1 fusion.50
  8.4 0.1 broadcast_in_dim.14
  8.5 0.1 fusion.47
  8.7 66.1 %shard_map.111 = (f32[4,2,1664]{2,1,0:T(2,128)S(1)}, f32[1536,256]{1,0:T(8,128)S(1)}, f32[256,1536]{1,0:T(8,128)S(1)}, f32[8,1536]{1,0:T(8,128)S(1)}, bf16[4,4,16,1664]{3,2,1,0:T(8,128)(2,1)S(1)}) custom-call(bf16[4,2,1536]{2,1,0:T(2,128)(2,1)S(1)} %bitcast.118, bf16[1536,256]{1,0:T(8,128)(2,1)S(1)} %bitcast.110, bf16[256,1536]{1,0:T(8,128)(2,1)S(1)} %bitcast.112, ...), custom_call_target="tpu_custom_call" | custom-call | tf_op jit(solution)/shard_map/pallas_call | solution.py:370
  74.7 0.0 copy-start.3
  74.7 1.1 copy-done.3
  75.9 0.9 copy-done.4
  76.8 0.1 slice_reduce_fusion.3
  76.9 0.1 fusion.3
  77.0 0.3 convolution_add_fusion.1
  77.3 0.4 fusion
  77.7 1.3 collective-permute-start
  79.0 14.9 %collective-permute-done = bf16[6,6144]{1,0:T(8,128)(2,1)} collective-permute-done((bf16[6,6144]{1,0:T(8,128)(2,1)S(1)}, bf16[6,6144]{1,0:T(8,128)(2,1)}, u32[]{:S(2)}, u32[]{:S(2)}) %collective-permute-start) | collective-permute-done | bytes 73760 | tf_op jit(solution)/shard_map/ppermute | solution.py:18
  93.9 1.0 convolution_convert_fusion
  95.0 0.0 copy-start.5
  95.0 1.1 copy-done.5
  96.1 57.7 %shard_map.112 = (f32[4,2,1664]{2,1,0:T(2,128)S(1)}, bf16[1536,256]{1,0:T(8,128)(2,1)S(1)}, bf16[256,1536]{1,0:T(8,128)(2,1)S(1)}, f32[4,8,1536]{2,1,0:T(8,128)S(1)}) custom-call(bf16[4,2,1536]{2,1,0:T(2,128)(2,1)S(1)} %bitcast.117, bf16[1536,256]{1,0:T(8,128)(2,1)S(1)} %bitcast.111, bf16[256,1536]{1,0:T(8,128)(2,1)S(1)} %bitcast.113, ...), custom_call_target="tpu_custom_call" | custom-call | tf_op jit(solution)/shard_map/pallas_call | solution.py:370
  153.8 0.1 slice_reduce_fusion.2
  153.9 0.1 fusion.4
  154.0 0.3 fusion.64
  154.4 1.3 fusion.10
  155.7 0.8 copy.15
  156.5 0.9 copy.31
  157.4 0.9 copy.32
  158.3 0.7 copy.33
  (20 shorter events, 0.2 us)
Async XLA Ops:
  0.6 5.1 %copy-start = (f32[1,6144,8]{1,2,0:T(8,128)S(1)}, f32[1,6144,8]{1,2,0:T(8,128)}, u32[]{:S(2)}) copy-start(f32[1,6144,8]{1,2,0:T(8,128)} %param.13) | copy-start | bytes 589828
  0.6 7.4 %copy-start.6 = (bf16[1,6,6144]{2,1,0:T(8,128)(2,1)S(1)}, bf16[1,6,6144]{2,1,0:T(8,128)(2,1)}, u32[]{:S(2)}) copy-start(bf16[1,6,6144]{2,1,0:T(8,128)(2,1)} %param.9) | copy-start | bytes 221188
  0.7 8.0 %copy-start.2 = (bf16[1,1,256,1536]{3,2,1,0:T(8,128)(2,1)S(1)}, bf16[1,1,256,1536]{3,2,1,0:T(8,128)(2,1)}, u32[]{:S(2)}) copy-start(bf16[1,1,256,1536]{3,2,1,0:T(8,128)(2,1)} %param.15) | copy-start | bytes 2359300
  0.7 8.0 %copy-start.1 = (bf16[1,1,1536,256]{3,2,1,0:T(8,128)(2,1)S(1)}, bf16[1,1,1536,256]{3,2,1,0:T(8,128)(2,1)}, u32[]{:S(2)}) copy-start(bf16[1,1,1536,256]{3,2,1,0:T(8,128)(2,1)} %param.14) | copy-start | bytes 2359300
  74.7 1.2 copy-start.3
  75.9 0.9 copy-start.4
  77.7 16.2 %collective-permute-start = (bf16[6,6144]{1,0:T(8,128)(2,1)S(1)}, bf16[6,6144]{1,0:T(8,128)(2,1)}, u32[]{:S(2)}, u32[]{:S(2)}) collective-permute-start(bf16[6,6144]{1,0:T(8,128)(2,1)S(1)} %fusion), channel_id=1, source_target_pairs={{1,0},{2,1},{3,2},{5,4},{6,5},{7,6},{9,8},{10,9},{11,10},{13,12},{... | collective-permute-start | bytes 221192 | tf_op jit(solution)/shard_map/ppermute | solution.py:18
  95.0 1.2 copy-start.5
  96.1 58.2 %copy-start.7 = (bf16[6,6144]{1,0:T(8,128)(2,1)S(1)}, bf16[6,6144]{1,0:T(8,128)(2,1)}, u32[]{:S(2)}) copy-start(bf16[6,6144]{1,0:T(8,128)(2,1)} %param.10) | copy-start | bytes 221188

commit v3 on v2

v3 whole, which is shorter than its diff:
```python
import functools

import jax
import jax.numpy as jnp
from jax import lax
from jax.experimental import pallas as pl
from jax.experimental.pallas import tpu as pltpu
from jax.sharding import PartitionSpec as P

STEPS = 2
CAP = 2
EXT = 128


def rounded(value):
    return value.astype(jnp.bfloat16).astype(jnp.float32)


def split_ext(value):
    lanes = lax.broadcasted_iota(jnp.int32, value.shape[:-1] + (EXT,), len(value.shape) - 1)
    high = rounded(value)
    return jnp.where(lanes < EXT // 2, high, value - high)


def window_kernel(part, hidden, experts, sections, names, *refs):
    ref = dict(zip(names, refs))
    w_in, w_out = ref["w_in"], ref["w_out"]
    send, recv, own = ref["send"], ref["recv"], ref["own"]
    wide = part + EXT
    f32, bf16 = jnp.float32, jnp.bfloat16
    me = lax.axis_index("dp")
    section = lax.axis_index("section")
    before, after = (section + sections - 1) % sections, (section + 1) % sections
    line = me % 8
    base = me - line
    core = me % 2
    odd = (me // 2) % 2
    half = line // 4
    quarter = me % 4
    xpos = (me // 8) % 4
    zpos = me // 32
    ahead, behind, across = (xpos + 1) % 4, (xpos + 3) % 4, (xpos + 2) % 4

    def near_dev(r):
        return base + (line + r) % 8

    def z_dev(r):
        return ((zpos + r) % 4) * 32 + xpos * 8 + line

    def x_dev(r):
        return zpos * 32 + ((xpos + r) % 4) * 8 + line

    core_dev = base + (line // 2) * 2 + (1 - core)
    odd_dev = base + half * 4 + (1 - odd) * 2 + core
    half_dev = base + (line + 4) % 8

    barrier = pltpu.get_barrier_semaphore()
    peers = [near_dev(r) for r in range(1, 8)]
    peers += [z_dev(r) for r in range(1, 4)] + [x_dev(r) for r in range(1, 4)]
    for peer in peers:
        pl.semaphore_signal(barrier, inc=1, device_id={"dp": peer}, device_id_type=pl.DeviceIdType.MESH)
    for neighbour in (before, after):
        pl.semaphore_signal(
            barrier, inc=1, device_id={"section": neighbour}, device_id_type=pl.DeviceIdType.MESH)
    pl.semaphore_wait(barrier, len(peers) + 2)

    def copy(src, dst, slot, device):
        return pltpu.make_async_remote_copy(
            src_ref=src, dst_ref=dst, send_sem=send.at[slot], recv_sem=recv.at[slot],
            device_id={"dp": device}, device_id_type=pl.DeviceIdType.MESH)

    def copy_section(src, dst, slot, target):
        return pltpu.make_async_remote_copy(
            src_ref=src, dst_ref=dst, send_sem=send.at[slot], recv_sem=recv.at[slot],
            device_id={"section": target}, device_id_type=pl.DeviceIdType.MESH)

    sent, taken, kept = [], [0], [0]

    def slots(count):
        taken[0] += count
        return list(range(taken[0] - count, taken[0]))

    def go(src, dst, slot, device):
        c = copy(src, dst, slot, device)
        c.start()
        sent.append(c)

    def keep(src, dst):
        c = pltpu.make_async_copy(src, dst, own.at[kept[0]])
        kept[0] += 1
        c.start()
        return c

    class Gather:
        def __init__(self, pay, near, rows, columns):
            self.pay, self.near, self.rows, self.columns = pay, near, rows, columns
            self.n, self.z, self.x = slots(7), slots(3), slots(6)

        def near_start(self):
            self.mine = keep(self.pay.at[quarter], self.near.at[line])
            for r in range(1, 8):
                go(self.pay.at[(line + r) % 4], self.near.at[line], self.n[r - 1], near_dev(r))

        def near_wait(self):
            self.mine.wait()
            for r in range(1, 8):
                copy(self.pay.at[0], self.near.at[(line + 8 - r) % 8], self.n[r - 1], near_dev(r)).wait_recv()
            for at in range(0, self.columns, 512):
                size = min(512, self.columns - at)
                index = lax.broadcasted_iota(jnp.int32, (16, size), 0)
                block = jnp.zeros((16, size), f32)
                for s in range(8):
                    pair = self.near[s, :, at:at + size].astype(f32)
                    for k in range(2):
                        block = jnp.where(index == 2 * s + k, pair[k:k + 1], block)
                self.rows[zpos, xpos, :, at:at + size] = block.astype(bf16)

        def z_start(self):
            for r in range(1, 4):
                go(self.rows.at[zpos, xpos], self.rows.at[zpos, xpos], self.z[r - 1], z_dev(r))

        def z_wait(self):
            for r in range(1, 4):
                copy(self.rows.at[zpos, xpos], self.rows.at[(zpos + 4 - r) % 4, xpos], self.z[r - 1], z_dev(r)).wait_recv()

        def piece(self, top, x):
            return self.rows.at[pl.ds(2 * top, 2), x]

        def x_start(self):
            go(self.piece(0, xpos), self.piece(0, xpos), self.x[0], x_dev(1))
            go(self.piece(1, xpos), self.piece(1, xpos), self.x[1], x_dev(3))
            go(self.piece(1, xpos), self.piece(1, xpos), self.x[2], x_dev(1))
            go(self.piece(0, xpos), self.piece(0, xpos), self.x[3], x_dev(3))

        def x_pass(self):
            copy(self.piece(0, xpos), self.piece(0, behind), self.x[0], x_dev(1)).wait_recv()
            go(self.piece(0, behind), self.piece(0, behind), self.x[4], x_dev(1))
            copy(self.piece(1, xpos), self.piece(1, ahead), self.x[1], x_dev(3)).wait_recv()
            go(self.piece(1, ahead), self.piece(1, ahead), self.x[5], x_dev(3))

        def x_wait(self):
            copy(self.piece(1, xpos), self.piece(1, behind), self.x[2], x_dev(1)).wait_recv()
            copy(self.piece(0, xpos), self.piece(0, ahead), self.x[3], x_dev(3)).wait_recv()
            copy(self.piece(0, xpos), self.piece(0, across), self.x[4], x_dev(1)).wait_recv()
            copy(self.piece(1, xpos), self.piece(1, across), self.x[5], x_dev(3)).wait_recv()

    tabs, slopes, router_t, head = ref["tabs"], ref["slopes"], ref["router_t"], ref["head"]
    is_last = section == sections - 1
    s_tab, s_rows, s_full = slots(3)
    c = copy_section(tabs.at[1], ref["tab_next"], s_tab, after)
    c.start()
    sent.append(c)
    gx = Gather(ref["pay_x"], ref["nx"], ref["xr"], wide)
    later = Gather(ref["pay_l"], ref["nl"], ref["lr"], wide)

    def slot_rows(table, rows):
        picked = [jnp.sum(table[:, c:c + 1] * rows, axis=0, keepdims=True) for c in range(CAP)]
        index = lax.broadcasted_iota(jnp.int32, (CAP, part), 0)
        return jnp.where(index == 0, picked[0], picked[1]).astype(bf16)

    def finish(step, dy, out):
        rf = ref[f"rf{step}"]
        dgate = rf[0, :, part:wide] + rf[4, :, part:wide]
        for q in range(4):
            rows = rf[q, :, 0:part] + rf[q + 4, :, 0:part]
            result = dy(q)
            for c in range(CAP):
                dlog = slopes[step, :, c:c + 1] * dgate[c:c + 1, 0:1]
                row = rows[c:c + 1] + jnp.sum(dlog * router_t[q], axis=0, keepdims=True)
                result = result + tabs[step, :, c:c + 1] * row
            out[q] = result.astype(bf16)

    def one_step(step):
        first_step = step == 0
        local_ref = lambda name: ref[f"{name}{step}"]
        ys = local_ref("yr")
        gy = Gather(ref["pay_y"] if first_step else ref["pay1"], local_ref("ny"), ys, part)
        xs = ref["xr"] if first_step else ref["lr"]
        now = (gx, gy) if first_step else (gy,)
        for g in now:
            g.near_start()
        if first_step:
            later.near_start()
        for g in now:
            g.near_wait()
            g.z_start()
        if first_step:
            later.near_wait()
        for g in now:
            g.z_wait()
            g.x_start()
        if first_step:
            later.z_start()
        else:
            c = copy_section(ref["res0"], ref["inc"], s_full, before)
            c.start()
            sent.append(c)
        for g in now:
            g.x_pass()
        for g in now:
            g.x_wait()
        if first_step:
            later.z_wait()
            later.x_start()

        xmat = xs[:, :, :, 0:part].reshape(256, part)
        pu, ra, sb, rb, dd = local_ref("pu"), local_ref("ra"), local_ref("sb"), local_ref("rb"), local_ref("dd")
        pre = jnp.dot(xmat, w_in[...], preferred_element_type=f32)
        pu[:, :, 0:hidden] = pre.reshape(4, 64, hidden)
        upper = lax.dot_general(ys[...].reshape(256, part), w_out[...], (((1,), (1,)), ((), ())), preferred_element_type=f32)
        pu[:, :, hidden:2 * hidden] = upper.reshape(4, 64, hidden)

        s1, s2, s3, s4 = slots(4)
        go(pu.at[pl.ds(2 * (1 - core), 2)], ra, s1, core_dev)
        copy(pu.at[pl.ds(2 * (1 - core), 2)], ra, s1, core_dev).wait_recv()
        sb[...] = pu[pl.ds(2 * core, 2)] + ra[...]
        go(sb.at[1 - odd], rb, s2, odd_dev)
        if first_step:
            later.x_pass()
        copy(sb.at[1 - odd], rb, s2, odd_dev).wait_recv()
        k = 2 * core + odd
        both = sb[odd] + rb[...]
        pre = both[:, 0:hidden]
        upper = both[:, hidden:2 * hidden]
        gate = xs[k, :, :, part:wide].reshape(64, EXT).astype(f32)[:, 0:1]
        sig = jax.nn.sigmoid(pre)
        act = pre * sig
        dd[k, :, 0:hidden] = (gate * upper * (sig * (1.0 + pre * (1.0 - sig)))).astype(bf16)
        dd[k, :, hidden:2 * hidden] = (gate * act).astype(bf16)
        sums = jnp.sum(act * upper, axis=1, keepdims=True)
        dd[k, :, 2 * hidden:2 * hidden + EXT] = jnp.broadcast_to(sums, (64, EXT)).astype(bf16)
        go(dd.at[k], dd.at[k], s3, odd_dev)
        copy(dd.at[k], dd.at[2 * core + 1 - odd], s3, odd_dev).wait_recv()
        go(dd.at[pl.ds(2 * core, 2)], dd.at[pl.ds(2 * core, 2)], s4, core_dev)
        copy(dd.at[pl.ds(2 * core, 2)], dd.at[pl.ds(2 * (1 - core), 2)], s4, core_dev).wait_recv()

        ax, az, ah = local_ref("ax"), local_ref("az"), local_ref("ah")
        sums = dd[:, :, 2 * hidden:2 * hidden + EXT].reshape(256, EXT)
        pick = (lax.broadcasted_iota(jnp.int32, (16, EXT), 1) == 0).astype(f32).astype(bf16)
        ax[xpos] = lax.dot_general(pick, sums, (((1,), (1,)), ((), ())), preferred_element_type=f32)[0:8]
        sx, sz = slots(3), slots(3)
        sh, = slots(1)
        for r in range(1, 4):
            go(ax.at[xpos], ax.at[xpos], sx[r - 1], x_dev(r))

        dx, rx, ry, dz, rz = local_ref("dx"), local_ref("rx"), local_ref("ry"), local_ref("dz"), local_ref("rz")
        dpre = dd[:, :, 0:hidden].reshape(256, hidden)
        scaled = dd[:, :, hidden:2 * hidden].reshape(256, hidden)
        term = lax.dot_general(dpre, w_in[...], (((1,), (1,)), ((), ())), preferred_element_type=f32)
        dx[:, :, :, 0:part] = term.astype(bf16).reshape(4, 4, 16, part)
        lanes = lax.broadcasted_iota(jnp.int32, (256, EXT), 1)
        sums = jnp.where(lanes < EXT // 2, sums.astype(f32), 0.0)
        dx[:, :, :, part:wide] = sums.astype(bf16).reshape(4, 4, 16, EXT)

        def piece(top, x):
            return dx.at[pl.ds(2 * top, 2), x]

        if first_step:
            later.x_wait()
        b = slots(6)
        go(piece(0, across), ry.at[0], b[0], x_dev(1))
        go(piece(1, across), ry.at[1], b[1], x_dev(3))
        go(piece(1, ahead), rx.at[0, pl.ds(2, 2)], b[2], x_dev(1))
        go(piece(0, behind), rx.at[1, pl.ds(0, 2)], b[3], x_dev(3))
        for r in range(1, 4):
            copy(ax.at[xpos], ax.at[(xpos + 4 - r) % 4], sx[r - 1], x_dev(r)).wait_recv()
        az[zpos] = ax[0] + ax[1] + ax[2] + ax[3]
        for r in range(1, 4):
            go(az.at[zpos], az.at[zpos], sz[r - 1], z_dev(r))

        def joined(first, second):
            value = first.astype(f32) + second.astype(f32)
            column = value[..., part:part + 1] + value[..., part + EXT // 2:part + EXT // 2 + 1]
            return value[..., 0:part].astype(bf16), split_ext(column).astype(bf16)

        def pass_on(top, x, slot, came, device):
            copy(piece(top, x), ry.at[came], slot, device).wait_recv()
            for z in range(2):
                main, ext = joined(dx[2 * top + z, x], ry[came, z])
                dx[2 * top + z, x, :, 0:part] = main
                dx[2 * top + z, x, :, part:wide] = ext

        pass_on(0, ahead, b[0], 0, x_dev(1))
        go(piece(0, ahead), rx.at[0, pl.ds(0, 2)], b[4], x_dev(1))
        pass_on(1, behind, b[1], 1, x_dev(3))
        go(piece(1, behind), rx.at[1, pl.ds(2, 2)], b[5], x_dev(3))
        one = lax.dot_general(xmat, dpre, (((0,), (0,)), ((), ())), preferred_element_type=f32)
        two = lax.dot_general(scaled, ys[...].reshape(256, part), (((0,), (0,)), ((), ())), preferred_element_type=f32)
        if first_step:
            ref["acc_in"][...] = one
            ref["acc_out"][...] = two
        else:
            ref["gin"][...] = (ref["acc_in"][...] + one).astype(bf16)
            ref["gout"][...] = (ref["acc_out"][...] + two).astype(bf16)
        for r in range(1, 4):
            copy(az.at[zpos], az.at[(zpos + 4 - r) % 4], sz[r - 1], z_dev(r)).wait_recv()
        ah[half] = az[0] + az[1] + az[2] + az[3]
        go(ah.at[half], ah.at[half], sh, half_dev)
        copy(piece(1, xpos), rx.at[0, pl.ds(2, 2)], b[2], x_dev(1)).wait_recv()
        copy(piece(0, xpos), rx.at[1, pl.ds(0, 2)], b[3], x_dev(3)).wait_recv()
        copy(piece(0, xpos), rx.at[0, pl.ds(0, 2)], b[4], x_dev(1)).wait_recv()
        copy(piece(1, xpos), rx.at[1, pl.ds(2, 2)], b[5], x_dev(3)).wait_recv()
        for z in range(4):
            value = dx[z, xpos].astype(f32) + rx[0, z].astype(f32) + rx[1, z].astype(f32)
            dz[z, :, 0:part] = value[:, 0:part].astype(bf16)
            column = value[:, part:part + 1] + value[:, part + EXT // 2:part + EXT // 2 + 1]
            dz[z, :, part:wide] = split_ext(column).astype(bf16)
        e = slots(3)
        for r in range(1, 4):
            go(dz.at[(zpos + r) % 4], rz.at[r - 1], e[r - 1], z_dev(r))
        copy(ah.at[half], ah.at[1 - half], sh, half_dev).wait_recv()
        dgate = (ah[0] + ah[1])[0:1]
        ext = jnp.transpose(xs[:, :, :, part:wide].reshape(256, EXT).astype(f32))
        slope = ext[8:16] + ext[16:24] + ext[24:32]
        dlog = slope * dgate
        high = rounded(dlog)
        middle = rounded(dlog - high)
        split = jnp.concatenate([high, middle, dlog - high - middle, jnp.zeros_like(high)], axis=0).astype(bf16)
        router = jnp.dot(split, xmat, preferred_element_type=f32)
        router = router[0:8] + router[8:16] + router[16:24]
        if first_step:
            ref["acc_router"][...] = router
        else:
            mine, parts = ref["mine"], ref["parts"]
            mine[...] = ref["acc_router"][...] + router
            held = keep(mine, parts.at[quarter])
            qs = slots(3)
            for r in range(1, 4):
                go(mine, parts.at[quarter], qs[r - 1], base + half * 4 + (quarter + r) % 4)
        for r in range(1, 4):
            copy(dz.at[0], rz.at[r - 1], e[r - 1], z_dev(r)).wait_recv()
        fin, split, rf = local_ref("fin"), local_ref("split"), local_ref("rf")
        value = dz[zpos].astype(f32)
        for r in range(3):
            value = value + rz[r].astype(f32)
        fin[:, 0:part] = value[:, 0:part]
        column = value[:, part:part + 1] + value[:, part + EXT // 2:part + EXT // 2 + 1]
        fin[:, part:wide] = jnp.broadcast_to(column, (16, EXT))
        for s in range(8):
            split[s] = fin[2 * s:2 * s + 2, :]
        stay = keep(split.at[line], rf.at[line])
        n = slots(7)
        for r in range(1, 8):
            go(split.at[(line + r) % 8], rf.at[line], n[r - 1], near_dev(r))
        stay.wait()
        for r in range(1, 8):
            copy(split.at[0], rf.at[(line + 8 - r) % 8], n[r - 1], near_dev(r)).wait_recv()
        if not first_step:
            held.wait()
            for r in range(1, 4):
                copy(mine, parts.at[(quarter + 4 - r) % 4], qs[r - 1], core_dev).wait_recv()
            ref["gr"][...] = parts[...]

    one_step(0)
    res0 = ref["res0"]
    finish(0, lambda q: ref["dy0"][q], res0)
    copy_section(tabs.at[1], ref["tab_next"], s_tab, after).wait_recv()
    for q in range(4):
        ref["rows_out"][q] = slot_rows(ref["tab_next"][...], res0[q].astype(f32))
    c = copy_section(ref["rows_out"], ref["rows_in"], s_rows, before)
    c.start()
    sent.append(c)
    ref["out"][0] = res0[...]
    c.wait_recv()
    for q in range(4):
        own_rows = slot_rows(tabs[1], head[q]).astype(f32)
        ref["pay1"][q] = jnp.where(is_last, own_rows, ref["rows_in"][q].astype(f32)).astype(bf16)
    one_step(1)
    copy_section(res0, ref["inc"], s_full, before).wait_recv()
    live = tabs[1, :, CAP:CAP + 1] > 0.5
    finish(
        1,
        lambda q: jnp.where(live, jnp.where(is_last, head[q], ref["inc"][q].astype(f32)), 0.0),
        ref["out"].at[1],
    )
    for c in sent:
        c.wait_send()


def run_window(experts, sections, ins):
    part, hidden = ins["w_in"].shape
    wide = part + EXT
    bf16, f32 = jnp.bfloat16, jnp.float32
    tokens = ins["dy0"].shape[1]
    outs = {
        "out": ((STEPS, 4, tokens, part), bf16),
        "gin": ((part, hidden), bf16),
        "gout": ((hidden, part), bf16),
        "gr": ((4, experts, part), f32),
    }
    each = {
        "ny": ((8, CAP, part), bf16),
        "yr": ((4, 4, 16, part), bf16),
        "pu": ((4, 64, 2 * hidden), f32),
        "ra": ((2, 64, 2 * hidden), f32),
        "sb": ((2, 64, 2 * hidden), f32),
        "rb": ((64, 2 * hidden), f32),
        "dd": ((4, 64, 2 * hidden + EXT), bf16),
        "dx": ((4, 4, 16, wide), bf16),
        "rx": ((2, 4, 16, wide), bf16),
        "ry": ((2, 2, 16, wide), bf16),
        "dz": ((4, 16, wide), bf16),
        "rz": ((3, 16, wide), bf16),
        "ax": ((4, 8, 256), f32),
        "az": ((4, 8, 256), f32),
        "ah": ((2, 8, 256), f32),
        "fin": ((16, wide), f32),
        "split": ((8, CAP, wide), f32),
        "rf": ((8, CAP, wide), f32),
    }
    scratch = {f"{name}{step}": leaf for step in range(STEPS) for name, leaf in each.items()}
    scratch.update({
        "nx": ((8, CAP, wide), bf16),
        "nl": ((8, CAP, wide), bf16),
        "xr": ((4, 4, 16, wide), bf16),
        "lr": ((4, 4, 16, wide), bf16),
        "acc_in": ((part, hidden), f32),
        "acc_out": ((hidden, part), f32),
        "acc_router": ((experts, part), f32),
        "mine": ((experts, part), f32),
        "parts": ((4, experts, part), f32),
        "tab_next": ((tokens, 128), f32),
        "res0": ((4, tokens, part), bf16),
        "inc": ((4, tokens, part), bf16),
        "rows_out": ((4, CAP, part), bf16),
        "rows_in": ((4, CAP, part), bf16),
        "pay1": ((4, CAP, part), bf16),
    })
    names = list(ins) + list(outs) + list(scratch) + ["send", "recv", "own"]
    vmem = pl.BlockSpec(memory_space=pltpu.VMEM)
    copies = 160
    got = pl.pallas_call(
        functools.partial(window_kernel, part, hidden, experts, sections, names),
        out_shape=[jax.ShapeDtypeStruct(*leaf) for leaf in outs.values()],
        in_specs=[vmem] * len(ins),
        out_specs=[vmem] * len(outs),
        scratch_shapes=[pltpu.VMEM(*leaf) for leaf in scratch.values()]
        + [pltpu.SemaphoreType.DMA((copies,)), pltpu.SemaphoreType.DMA((copies,)), pltpu.SemaphoreType.DMA((8,))],
        compiler_params=pltpu.CompilerParams(
            collective_id=0, has_side_effects=True, vmem_limit_bytes=48 << 20
        ),
    )(*ins.values())
    return dict(zip(outs, got))


def local(saved_inputs, carried, head_grad, routing, replica_counts, router, w_in, w_out):
    hi = lax.Precision.HIGHEST
    section_index = lax.axis_index("section")
    dev_index = lax.axis_index("dp")
    width = head_grad.shape[1]
    part = w_in.shape[2]
    experts = router.shape[2]
    router_w = router[0]
    my_count = replica_counts[dev_index]
    first = (jnp.arange(experts) == 0).astype(jnp.float32)
    slots = jnp.arange(CAP, dtype=jnp.int32)

    def quarters(rows):
        return rows.reshape(CAP, 4, part).transpose(1, 0, 2)

    def prepare(step):
        xin = saved_inputs[0, step]
        ids = routing[0, step]
        live = step + section_index < my_count
        xf = xin.astype(jnp.float32)
        logits = jnp.dot(xf, router_w, precision=hi)
        expo = jnp.exp(logits)
        prob = expo / jnp.sum(expo, axis=1, keepdims=True)
        routed = ((ids[:, 0] == 0) | (ids[:, 1] == 0)) & live
        slot = jnp.cumsum(routed.astype(jnp.int32), dtype=jnp.int32) - 1
        table = ((slot[None, :] == slots[:, None]) & routed[None, :]).astype(jnp.float32)
        xs = jnp.dot(table.astype(jnp.bfloat16), xin, preferred_element_type=jnp.float32).astype(jnp.bfloat16)
        gate = jnp.dot(table, prob[:, 0], precision=hi).astype(jnp.bfloat16)
        slope = jnp.dot(table, prob[:, :1] * (first[None, :] - prob), precision=hi)
        high = rounded(slope)
        middle = rounded(slope - high)
        low = rounded(slope - high - middle)
        ext = jnp.concatenate(
            [jnp.broadcast_to(gate.astype(jnp.float32)[:, None], (CAP, 8)), high, middle, low], axis=1)
        ext = jnp.pad(ext, ((0, 0), (0, EXT - ext.shape[1]))).astype(jnp.bfloat16)
        payload = jnp.concatenate([quarters(xs), jnp.broadcast_to(ext[None], (4, CAP, EXT))], axis=2)
        column = jnp.concatenate([table.T, live.astype(jnp.float32) * jnp.ones((xin.shape[0], 1))], axis=1)
        column = jnp.pad(column, ((0, 0), (0, 128 - column.shape[1])))
        return (table, live, payload, column, jnp.pad(slope.T, ((0, 0), (0, 128 - CAP))))

    prepared = [prepare(step) for step in range(STEPS)]
    def token_quarters(rows):
        return rows.astype(jnp.float32).reshape(-1, 4, part).transpose(1, 0, 2)

    table, live, payload, *_ = prepared[0]
    dy = jnp.where(live, carried[0], jnp.zeros_like(carried[0]))
    ys = jnp.dot(table.astype(jnp.bfloat16), dy, preferred_element_type=jnp.float32).astype(jnp.bfloat16)
    got = run_window(experts, lax.axis_size("section"), {
        "w_in": w_in[0, 0],
        "w_out": w_out[0, 0],
        "pay_y": quarters(ys),
        "pay_x": payload,
        "pay_l": prepared[1][2],
        "dy0": token_quarters(dy),
        "head": token_quarters(head_grad),
        "tabs": jnp.stack([prepared[step][3] for step in range(STEPS)]),
        "slopes": jnp.stack([prepared[step][4] for step in range(STEPS)]),
        "router_t": router_w.T.reshape(experts, 4, part).transpose(1, 0, 2),
    })
    grad_router = got["gr"].transpose(0, 2, 1).reshape(width, experts)
    input_grad = got["out"].transpose(0, 2, 1, 3).reshape(STEPS, 1, -1, width)
    return (input_grad, got["gin"][None, None], got["gout"][None, None], grad_router[None])


def solution(mesh):
    in_specs = (
        P("section", None, "dp", None),
        P("section", "dp", None),
        P("dp", None),
        P("section", None, "dp", None),
        P(),
        P("section", None, None),
        P("section", "dp", None, None),
        P("section", "dp", None, None),
    )
    out_specs = (
        P(None, "section", "dp", None),
        P("section", "dp", None, None),
        P("section", "dp", None, None),
        P("section", None, None),
    )
    return jax.shard_map(local, mesh=mesh, in_specs=in_specs, out_specs=out_specs, check_vma=False)
```

time: 159 us -> 148 us (0.931)
  waiting for transfers between devices: 14.9 us -> 0 us
  Pallas kernels: 124 us -> 132 us
  local copies, waits for them, and re-layouts: 10.4 us -> 7.34 us
  matrix products: 5.62 us -> 2.62 us
  other arithmetic: 0.8 us -> 3.17 us
    ppermute x1 -> x0, waiting for transfers between devices: 14.9 us -> none  [shifted(): return lax.ppermute(array, axis, pairs)]
    pallas_call x2 -> x1, Pallas kernels: 124 us -> 132 us  [run_window(): pl.pallas_call(functools.partial(window_kernel, part, hidden, experts, se...]
    dot_general x8 -> x1, matrix products: 3.72 us -> 0.76 us  [local(): jnp.dot(table.astype(jnp.bfloat16), dy, preferred_element_type=jnp.float32)]
    unnamed x20 -> x23, local copies, waits for them, and re-layouts: 6.49 us -> 5.18 us
  transfers between devices with their start and end apart: 1 -> 0, of which waited for: 1 -> 0; matrix products, arithmetic and copies ran while one was open for 0% -> 0% of each run, Pallas kernels for 0% -> 0%
where the time goes in v3:
time: 148 us; the launch traced here: 147 us
  Pallas kernels  132 us (89%)
  local copies, waits for them, and re-layouts  7.34 us (5%)
  other arithmetic  3.17 us (2%)
  matrix products  2.62 us (2%)
  between operations  2.1 us (1%)
    pallas_call x1, Pallas kernels, run_window(): pl.pallas_call(functools.partial(window_kernel, part, hidden, experts, se...  132 us
    unnamed x23, local copies, waits for them, and re-layouts  5.18 us

profile of v3, /device:TPU:1, one launch (start us, length us, event | category | flops | bytes accessed | tf_op | source)
XLA Modules:
  0.0 146.7 jit_solution(15598991016309575875)
XLA Ops:
  0.6 0.0 copy-start.9
  0.6 0.6 copy-done.9
  1.3 0.6 dynamic_slice.3
  3.2 0.0 copy-start.8
  3.2 0.7 copy-done.8
  3.9 0.2 reduce-window.17
  4.1 0.2 reduce-window.16
  4.3 0.1 fusion.13
  4.3 0.1 fusion.14
  4.4 0.0 copy-start.6
  4.5 0.9 broadcast_select_fusion
  5.4 0.8 convolution_convert_fusion.2
  6.2 0.0 copy-done.6
  6.2 0.2 fusion.41
  6.4 0.7 copy-done
  7.1 0.4 fusion.45
  7.5 0.0 copy-start.1
  7.6 0.2 convolution_convert_fusion
  7.7 0.1 broadcast_divide_fusion
  7.8 0.1 slice_reduce_fusion
  7.9 0.2 fusion.42
  8.1 0.1 fusion.1
  8.2 0.1 broadcast_in_dim.17
  8.3 0.1 fusion.36
  8.4 0.7 pad_maximum_fusion.1.refs_4_
  9.1 0.1 copy.17
  9.1 0.4 fusion.44
  9.6 0.2 convolution_convert_fusion.1
  9.8 0.1 broadcast_divide_fusion.1
  9.8 0.1 slice_reduce_fusion.1
  10.0 0.2 fusion.43
  10.2 0.1 fusion
  10.3 0.1 broadcast_in_dim.15
  10.4 0.1 fusion.33
  10.5 0.7 pad_maximum_fusion.refs_3_
  11.1 0.1 copy.16
  11.2 0.0 copy-done.7
  11.2 0.0 copy-start.4
  11.2 0.0 copy-start.5
  11.3 0.7 copy-done.3
  11.9 0.0 copy-done.4
  12.0 0.0 copy-done.5
  12.0 131.5 %shard_map.111 = (bf16[2,4,6,1536]{3,2,1,0:T(8,128)(2,1)S(1)}, bf16[1536,256]{1,0:T(8,128)(2,1)S(1)}, bf16[256,1536]{1,0:T(8,128)(2,1)S(1)}, f32[4,8,1536]{2,1,0:T(8,128)S(1)}) custom-call(bf16[1536,256]{1,0:T(8,128)(2,1)S(1)} %bitcast.95, bf16[256,1536]{1,0:T(8,128)(2,1)S(1)} %bitcast.96, bf16[4,2,1536]{2,1,0:T(2,128)(2,1)S(1)} %bitcast.101, ...), custom_call_target="tpu_custom_call" | custom-call | tf_op jit(solution)/shard_map/pallas_call | solution.py:432
  143.5 0.1 copy.18
  143.6 0.7 reshape.135
  144.3 0.9 copy.34
  145.2 0.9 copy.35
  146.1 0.7 copy.36
  (21 shorter events, 0.1 us)
Async XLA Ops:
  0.6 0.7 copy-start.9
  3.2 0.7 copy-start.8
  4.4 1.7 %copy-start.6 = (bf16[1,2,6,6144]{3,1,2,0:T(2,128)(2,1)S(1)}, bf16[1,2,6,6144]{3,1,2,0:T(2,128)(2,1)}, u32[]{:S(2)}) copy-start(bf16[1,2,6,6144]{3,1,2,0:T(2,128)(2,1)} %param.8) | copy-start | bytes 442372
  6.2 0.9 copy-start
  7.1 4.1 %copy-start.7 = (bf16[6,6144]{1,0:T(8,128)(2,1)S(1)}, bf16[6,6144]{1,0:T(8,128)(2,1)}, u32[]{:S(2)}) copy-start(bf16[6,6144]{1,0:T(8,128)(2,1)} %param.10) | copy-start | bytes 221188
  7.1 4.2 %copy-start.2 = (bf16[1,1,256,1536]{3,2,1,0:T(8,128)(2,1)S(1)}, bf16[1,1,256,1536]{3,2,1,0:T(8,128)(2,1)}, u32[]{:S(2)}) copy-start(bf16[1,1,256,1536]{3,2,1,0:T(8,128)(2,1)} %param.15) | copy-start | bytes 2359300
  7.5 3.7 %copy-start.1 = (bf16[1,1,1536,256]{3,2,1,0:T(8,128)(2,1)S(1)}, bf16[1,1,1536,256]{3,2,1,0:T(8,128)(2,1)}, u32[]{:S(2)}) copy-start(bf16[1,1,1536,256]{3,2,1,0:T(8,128)(2,1)} %param.14) | copy-start | bytes 2359300
  11.2 0.7 copy-start.3
  11.2 0.8 copy-start.4
  11.2 0.8 copy-start.5

commit v4 on v3

--- a/solution.py
+++ b/solution.py
@@ -94,7 +94,7 @@
     class Gather:
         def __init__(self, pay, near, rows, columns):
             self.pay, self.near, self.rows, self.columns = pay, near, rows, columns
-            self.n, self.z, self.x = slots(7), slots(3), slots(6)
+            self.n, self.z, self.x = slots(7), slots(3), [slots(6), slots(6)]
 
         def near_start(self):
             self.mine = keep(self.pay.at[quarter], self.near.at[line])
@@ -123,26 +123,32 @@
             for r in range(1, 4):
                 copy(self.rows.at[zpos, xpos], self.rows.at[(zpos + 4 - r) % 4, xpos], self.z[r - 1], z_dev(r)).wait_recv()
 
-        def piece(self, top, x):
-            return self.rows.at[pl.ds(2 * top, 2), x]
-
-        def x_start(self):
-            go(self.piece(0, xpos), self.piece(0, xpos), self.x[0], x_dev(1))
-            go(self.piece(1, xpos), self.piece(1, xpos), self.x[1], x_dev(3))
-            go(self.piece(1, xpos), self.piece(1, xpos), self.x[2], x_dev(1))
-            go(self.piece(0, xpos), self.piece(0, xpos), self.x[3], x_dev(3))
-
-        def x_pass(self):
-            copy(self.piece(0, xpos), self.piece(0, behind), self.x[0], x_dev(1)).wait_recv()
-            go(self.piece(0, behind), self.piece(0, behind), self.x[4], x_dev(1))
-            copy(self.piece(1, xpos), self.piece(1, ahead), self.x[1], x_dev(3)).wait_recv()
-            go(self.piece(1, ahead), self.piece(1, ahead), self.x[5], x_dev(3))
-
-        def x_wait(self):
-            copy(self.piece(1, xpos), self.piece(1, behind), self.x[2], x_dev(1)).wait_recv()
-            copy(self.piece(0, xpos), self.piece(0, ahead), self.x[3], x_dev(3)).wait_recv()
-            copy(self.piece(0, xpos), self.piece(0, across), self.x[4], x_dev(1)).wait_recv()
-            copy(self.piece(1, xpos), self.piece(1, across), self.x[5], x_dev(3)).wait_recv()
+        def piece(self, t, top, x):
+            return self.rows.at[2 * t + top, x]
+
+        def came(self, t, top, x, slot, device):
+            copy(self.piece(t, top, xpos), self.piece(t, top, x), self.x[t][slot], device).wait_recv()
+
+        def give(self, t, top, x, slot, device):
+            go(self.piece(t, top, x), self.piece(t, top, x), self.x[t][slot], device)
+
+        def x_start(self, t):
+            self.give(t, 0, xpos, 0, x_dev(1))
+            self.give(t, 1, xpos, 1, x_dev(3))
+            self.give(t, 1, xpos, 2, x_dev(1))
+            self.give(t, 0, xpos, 3, x_dev(3))
+
+        def x_pass(self, t):
+            self.came(t, 0, behind, 0, x_dev(1))
+            self.give(t, 0, behind, 4, x_dev(1))
+            self.came(t, 1, ahead, 1, x_dev(3))
+            self.give(t, 1, ahead, 5, x_dev(3))
+
+        def x_wait(self, t):
+            self.came(t, 1, behind, 2, x_dev(1))
+            self.came(t, 0, ahead, 3, x_dev(3))
+            self.came(t, 0, across, 4, x_dev(1))
+            self.came(t, 1, across, 5, x_dev(3))
 
     tabs, slopes, router_t, head = ref["tabs"], ref["slopes"], ref["router_t"], ref["head"]
     is_last = section == sections - 1
@@ -188,54 +194,93 @@
             later.near_wait()
         for g in now:
             g.z_wait()
-            g.x_start()
+        for t in range(2):
+            for g in now:
+                g.x_start(t)
         if first_step:
             later.z_start()
         else:
             c = copy_section(ref["res0"], ref["inc"], s_full, before)
             c.start()
             sent.append(c)
-        for g in now:
-            g.x_pass()
-        for g in now:
-            g.x_wait()
+        for t in range(2):
+            for g in now:
+                g.x_pass(t)
+
+        pu, ra, sb, rb, dd = (local_ref(name) for name in ("pu", "ra", "sb", "rb", "dd"))
+        s1, s2, s3, s4 = slots(2), slots(2), slots(2), slots(2)
+
+        def ends_half(t):
+            for g in now:
+                g.x_wait(t)
+            if not first_step:
+                later.x_wait(t)
+            pre = jnp.dot(xs[2 * t:2 * t + 2, :, :, 0:part].reshape(128, part), w_in[...], preferred_element_type=f32)
+            pu[t, :, :, 0:hidden] = pre.reshape(4, 32, hidden)
+            upper = lax.dot_general(
+                ys[2 * t:2 * t + 2].reshape(128, part), w_out[...], (((1,), (1,)), ((), ())), preferred_element_type=f32)
+            pu[t, :, :, hidden:2 * hidden] = upper.reshape(4, 32, hidden)
+            go(pu.at[t, pl.ds(2 * (1 - core), 2)], ra.at[t], s1[t], core_dev)
+
+        for t in range(2):
+            ends_half(t)
         if first_step:
             later.z_wait()
-            later.x_start()
-
+            for t in range(2):
+                later.x_start(t)
+        for t in range(2):
+            copy(pu.at[t, pl.ds(2 * (1 - core), 2)], ra.at[t], s1[t], core_dev).wait_recv()
+            sb[t] = pu[t, pl.ds(2 * core, 2)] + ra[t]
+            go(sb.at[t, 1 - odd], rb.at[t], s2[t], odd_dev)
+        k = 2 * core + odd
+        for t in range(2):
+            copy(sb.at[t, 1 - odd], rb.at[t], s2[t], odd_dev).wait_recv()
+            both = sb[t, odd] + rb[t]
+            pre = both[:, 0:hidden]
+            upper = both[:, hidden:2 * hidden]
+            gate = xs[2 * t + core, pl.ds(2 * odd, 2), :, part:wide].reshape(32, EXT).astype(f32)[:, 0:1]
+            sig = jax.nn.sigmoid(pre)
+            act = pre * sig
+            dd[t, k, :, 0:hidden] = (gate * upper * (sig * (1.0 + pre * (1.0 - sig)))).astype(bf16)
+            dd[t, k, :, hidden:2 * hidden] = (gate * act).astype(bf16)
+            sums = jnp.sum(act * upper, axis=1, keepdims=True)
+            dd[t, k, :, 2 * hidden:2 * hidden + EXT] = jnp.broadcast_to(sums, (32, EXT)).astype(bf16)
+            go(dd.at[t, k], dd.at[t, k], s3[t], odd_dev)
+        if first_step:
+            for t in range(2):
+                later.x_pass(t)
+        for t in range(2):
+            copy(dd.at[t, k], dd.at[t, 2 * core + 1 - odd], s3[t], odd_dev).wait_recv()
+            pair = dd.at[t, pl.ds(2 * core, 2)]
+            go(pair, pair, s4[t], core_dev)
+
+        dx, rx, ry, dz, rz = (local_ref(name) for name in ("dx", "rx", "ry", "dz", "rz"))
+        b = [slots(6), slots(6)]
+
+        def piece(t, top, x):
+            return dx.at[2 * t + top, x]
+
+        def dx_half(t):
+            pair = dd.at[t, pl.ds(2 * core, 2)]
+            copy(pair, dd.at[t, pl.ds(2 * (1 - core), 2)], s4[t], core_dev).wait_recv()
+            dpre = dd[t, :, :, 0:hidden].reshape(128, hidden)
+            term = lax.dot_general(dpre, w_in[...], (((1,), (1,)), ((), ())), preferred_element_type=f32)
+            dx[2 * t:2 * t + 2, :, :, 0:part] = term.astype(bf16).reshape(2, 4, 16, part)
+            sums = dd[t, :, :, 2 * hidden:2 * hidden + EXT].reshape(128, EXT)
+            lanes = lax.broadcasted_iota(jnp.int32, (128, EXT), 1)
+            sums = jnp.where(lanes < EXT // 2, sums.astype(f32), 0.0)
+            dx[2 * t:2 * t + 2, :, :, part:wide] = sums.astype(bf16).reshape(2, 4, 16, EXT)
+            go(piece(t, 0, across), ry.at[t, 0], b[t][0], x_dev(1))
+            go(piece(t, 1, across), ry.at[t, 1], b[t][1], x_dev(3))
+            go(piece(t, 1, ahead), rx.at[0, 2 * t + 1], b[t][2], x_dev(1))
+            go(piece(t, 0, behind), rx.at[1, 2 * t], b[t][3], x_dev(3))
+
+        for t in range(2):
+            dx_half(t)
         xmat = xs[:, :, :, 0:part].reshape(256, part)
-        pu, ra, sb, rb, dd = local_ref("pu"), local_ref("ra"), local_ref("sb"), local_ref("rb"), local_ref("dd")
-        pre = jnp.dot(xmat, w_in[...], preferred_element_type=f32)
-        pu[:, :, 0:hidden] = pre.reshape(4, 64, hidden)
-        upper = lax.dot_general(ys[...].reshape(256, part), w_out[...], (((1,), (1,)), ((), ())), preferred_element_type=f32)
-        pu[:, :, hidden:2 * hidden] = upper.reshape(4, 64, hidden)
-
-        s1, s2, s3, s4 = slots(4)
-        go(pu.at[pl.ds(2 * (1 - core), 2)], ra, s1, core_dev)
-        copy(pu.at[pl.ds(2 * (1 - core), 2)], ra, s1, core_dev).wait_recv()
-        sb[...] = pu[pl.ds(2 * core, 2)] + ra[...]
-        go(sb.at[1 - odd], rb, s2, odd_dev)
-        if first_step:
-            later.x_pass()
-        copy(sb.at[1 - odd], rb, s2, odd_dev).wait_recv()
-        k = 2 * core + odd
-        both = sb[odd] + rb[...]
-        pre = both[:, 0:hidden]
-        upper = both[:, hidden:2 * hidden]
-        gate = xs[k, :, :, part:wide].reshape(64, EXT).astype(f32)[:, 0:1]
-        sig = jax.nn.sigmoid(pre)
-        act = pre * sig
-        dd[k, :, 0:hidden] = (gate * upper * (sig * (1.0 + pre * (1.0 - sig)))).astype(bf16)
-        dd[k, :, hidden:2 * hidden] = (gate * act).astype(bf16)
-        sums = jnp.sum(act * upper, axis=1, keepdims=True)
-        dd[k, :, 2 * hidden:2 * hidden + EXT] = jnp.broadcast_to(sums, (64, EXT)).astype(bf16)
-        go(dd.at[k], dd.at[k], s3, odd_dev)
-        copy(dd.at[k], dd.at[2 * core + 1 - odd], s3, odd_dev).wait_recv()
-        go(dd.at[pl.ds(2 * core, 2)], dd.at[pl.ds(2 * core, 2)], s4, core_dev)
-        copy(dd.at[pl.ds(2 * core, 2)], dd.at[pl.ds(2 * (1 - core), 2)], s4, core_dev).wait_recv()
 
         ax, az, ah = local_ref("ax"), local_ref("az"), local_ref("ah")
-        sums = dd[:, :, 2 * hidden:2 * hidden + EXT].reshape(256, EXT)
+        sums = dd[:, :, :, 2 * hidden:2 * hidden + EXT].reshape(256, EXT)
         pick = (lax.broadcasted_iota(jnp.int32, (16, EXT), 1) == 0).astype(f32).astype(bf16)
         ax[xpos] = lax.dot_general(pick, sums, (((1,), (1,)), ((), ())), preferred_element_type=f32)[0:8]
         sx, sz = slots(3), slots(3)
@@ -243,47 +288,30 @@
         for r in range(1, 4):
             go(ax.at[xpos], ax.at[xpos], sx[r - 1], x_dev(r))
 
-        dx, rx, ry, dz, rz = local_ref("dx"), local_ref("rx"), local_ref("ry"), local_ref("dz"), local_ref("rz")
-        dpre = dd[:, :, 0:hidden].reshape(256, hidden)
-        scaled = dd[:, :, hidden:2 * hidden].reshape(256, hidden)
-        term = lax.dot_general(dpre, w_in[...], (((1,), (1,)), ((), ())), preferred_element_type=f32)
-        dx[:, :, :, 0:part] = term.astype(bf16).reshape(4, 4, 16, part)
-        lanes = lax.broadcasted_iota(jnp.int32, (256, EXT), 1)
-        sums = jnp.where(lanes < EXT // 2, sums.astype(f32), 0.0)
-        dx[:, :, :, part:wide] = sums.astype(bf16).reshape(4, 4, 16, EXT)
-
-        def piece(top, x):
-            return dx.at[pl.ds(2 * top, 2), x]
-
-        if first_step:
-            later.x_wait()
-        b = slots(6)
-        go(piece(0, across), ry.at[0], b[0], x_dev(1))
-        go(piece(1, across), ry.at[1], b[1], x_dev(3))
-        go(piece(1, ahead), rx.at[0, pl.ds(2, 2)], b[2], x_dev(1))
-        go(piece(0, behind), rx.at[1, pl.ds(0, 2)], b[3], x_dev(3))
+        dpre = dd[:, :, :, 0:hidden].reshape(256, hidden)
+        scaled = dd[:, :, :, hidden:2 * hidden].reshape(256, hidden)
+
+        def joined(first, second):
+            value = first.astype(f32) + second.astype(f32)
+            column = value[..., part:part + 1] + value[..., part + EXT // 2:part + EXT // 2 + 1]
+            return value[..., 0:part].astype(bf16), split_ext(column).astype(bf16)
+
+        def pass_on(t, top, x, device, slot, side):
+            z = 2 * t + top
+            copy(piece(t, top, x), ry.at[t, top], b[t][top], device).wait_recv()
+            main, ext = joined(dx[z, x], ry[t, top])
+            dx[z, x, :, 0:part] = main
+            dx[z, x, :, part:wide] = ext
+            go(piece(t, top, x), rx.at[side, z], b[t][slot], device)
+
+        for t in range(2):
+            pass_on(t, 0, ahead, x_dev(1), 4, 0)
+            pass_on(t, 1, behind, x_dev(3), 5, 1)
         for r in range(1, 4):
             copy(ax.at[xpos], ax.at[(xpos + 4 - r) % 4], sx[r - 1], x_dev(r)).wait_recv()
         az[zpos] = ax[0] + ax[1] + ax[2] + ax[3]
         for r in range(1, 4):
             go(az.at[zpos], az.at[zpos], sz[r - 1], z_dev(r))
-
-        def joined(first, second):
-            value = first.astype(f32) + second.astype(f32)
-            column = value[..., part:part + 1] + value[..., part + EXT // 2:part + EXT // 2 + 1]
-            return value[..., 0:part].astype(bf16), split_ext(column).astype(bf16)
-
-        def pass_on(top, x, slot, came, device):
-            copy(piece(top, x), ry.at[came], slot, device).wait_recv()
-            for z in range(2):
-                main, ext = joined(dx[2 * top + z, x], ry[came, z])
-                dx[2 * top + z, x, :, 0:part] = main
-                dx[2 * top + z, x, :, part:wide] = ext
-
-        pass_on(0, ahead, b[0], 0, x_dev(1))
-        go(piece(0, ahead), rx.at[0, pl.ds(0, 2)], b[4], x_dev(1))
-        pass_on(1, behind, b[1], 1, x_dev(3))
-        go(piece(1, behind), rx.at[1, pl.ds(2, 2)], b[5], x_dev(3))
         one = lax.dot_general(xmat, dpre, (((0,), (0,)), ((), ())), preferred_element_type=f32)
         two = lax.dot_general(scaled, ys[...].reshape(256, part), (((0,), (0,)), ((), ())), preferred_element_type=f32)
         if first_step:
@@ -292,22 +320,28 @@
         else:
             ref["gin"][...] = (ref["acc_in"][...] + one).astype(bf16)
             ref["gout"][...] = (ref["acc_out"][...] + two).astype(bf16)
+        e = slots(3)
+        for t in range(2):
+            low, high = 2 * t, 2 * t + 1
+            copy(piece(t, 1, xpos), rx.at[0, high], b[t][2], x_dev(1)).wait_recv()
+            copy(piece(t, 0, xpos), rx.at[1, low], b[t][3], x_dev(3)).wait_recv()
+            copy(piece(t, 0, xpos), rx.at[0, low], b[t][4], x_dev(1)).wait_recv()
+            copy(piece(t, 1, xpos), rx.at[1, high], b[t][5], x_dev(3)).wait_recv()
+            for z in (low, high):
+                value = dx[z, xpos].astype(f32) + rx[0, z].astype(f32) + rx[1, z].astype(f32)
+                dz[z, :, 0:part] = value[:, 0:part].astype(bf16)
+                column = value[:, part:part + 1] + value[:, part + EXT // 2:part + EXT // 2 + 1]
+                dz[z, :, part:wide] = split_ext(column).astype(bf16)
+            for r in range(1, 4):
+                target = (zpos + r) % 4
+                c = copy(dz.at[target], rz.at[r - 1], e[r - 1], z_dev(r))
+                pl.when(target // 2 == t)(c.start)
+                if t == 0:
+                    sent.append(c)
         for r in range(1, 4):
             copy(az.at[zpos], az.at[(zpos + 4 - r) % 4], sz[r - 1], z_dev(r)).wait_recv()
         ah[half] = az[0] + az[1] + az[2] + az[3]
         go(ah.at[half], ah.at[half], sh, half_dev)
-        copy(piece(1, xpos), rx.at[0, pl.ds(2, 2)], b[2], x_dev(1)).wait_recv()
-        copy(piece(0, xpos), rx.at[1, pl.ds(0, 2)], b[3], x_dev(3)).wait_recv()
-        copy(piece(0, xpos), rx.at[0, pl.ds(0, 2)], b[4], x_dev(1)).wait_recv()
-        copy(piece(1, xpos), rx.at[1, pl.ds(2, 2)], b[5], x_dev(3)).wait_recv()
-        for z in range(4):
-            value = dx[z, xpos].astype(f32) + rx[0, z].astype(f32) + rx[1, z].astype(f32)
-            dz[z, :, 0:part] = value[:, 0:part].astype(bf16)
-            column = value[:, part:part + 1] + value[:, part + EXT // 2:part + EXT // 2 + 1]
-            dz[z, :, part:wide] = split_ext(column).astype(bf16)
-        e = slots(3)
-        for r in range(1, 4):
-            go(dz.at[(zpos + r) % 4], rz.at[r - 1], e[r - 1], z_dev(r))
         copy(ah.at[half], ah.at[1 - half], sh, half_dev).wait_recv()
         dgate = (ah[0] + ah[1])[0:1]
         ext = jnp.transpose(xs[:, :, :, part:wide].reshape(256, EXT).astype(f32))
@@ -391,11 +425,11 @@
     each = {
         "ny": ((8, CAP, part), bf16),
         "yr": ((4, 4, 16, part), bf16),
-        "pu": ((4, 64, 2 * hidden), f32),
-        "ra": ((2, 64, 2 * hidden), f32),
-        "sb": ((2, 64, 2 * hidden), f32),
-        "rb": ((64, 2 * hidden), f32),
-        "dd": ((4, 64, 2 * hidden + EXT), bf16),
+        "pu": ((2, 4, 32, 2 * hidden), f32),
+        "ra": ((2, 2, 32, 2 * hidden), f32),
+        "sb": ((2, 2, 32, 2 * hidden), f32),
+        "rb": ((2, 32, 2 * hidden), f32),
+        "dd": ((2, 4, 32, 2 * hidden + EXT), bf16),
         "dx": ((4, 4, 16, wide), bf16),
         "rx": ((2, 4, 16, wide), bf16),
         "ry": ((2, 2, 16, wide), bf16),
@@ -428,7 +462,7 @@
     })
     names = list(ins) + list(outs) + list(scratch) + ["send", "recv", "own"]
     vmem = pl.BlockSpec(memory_space=pltpu.VMEM)
-    copies = 160
+    copies = 240
     got = pl.pallas_call(
         functools.partial(window_kernel, part, hidden, experts, sections, names),
         out_shape=[jax.ShapeDtypeStruct(*leaf) for leaf in outs.values()],

time: 148 us -> 150 us (1.014)
  Pallas kernels: 132 us -> 135 us
    pallas_call x1, Pallas kernels: 132 us -> 135 us  [run_window(): pl.pallas_call(functools.partial(window_kernel, part, hidden, experts, se...]
where the time goes in v4:
time: 150 us
  Pallas kernels  135 us (90%)
  local copies, waits for them, and re-layouts  7.34 us (5%)
  other arithmetic  3.17 us (2%)
  matrix products  2.62 us (2%)
  between operations  2.1 us (1%)
    pallas_call x1, Pallas kernels, run_window(): pl.pallas_call(functools.partial(window_kernel, part, hidden, experts, se...  135 us
    unnamed x23, local copies, waits for them, and re-layouts  5.18 us

profile of v4, /device:TPU:1, one launch (start us, length us, event | category | flops | bytes accessed | tf_op | source)
XLA Modules:
  0.0 150.1 jit_solution(7660656256214818312)
XLA Ops:
  0.6 0.0 copy-start.9
  0.6 0.6 copy-done.9
  1.3 0.6 dynamic_slice.3
  3.2 0.0 copy-start.8
  3.2 0.7 copy-done.8
  3.9 0.2 reduce-window.17
  4.1 0.2 reduce-window.16
  4.3 0.1 fusion.13
  4.3 0.1 fusion.14
  4.4 0.0 copy-start.6
  4.5 0.9 broadcast_select_fusion
  5.4 0.8 convolution_convert_fusion.2
  6.2 0.0 copy-done.6
  6.2 0.2 fusion.41
  6.4 0.7 copy-done
  7.1 0.4 fusion.45
  7.5 0.0 copy-start.1
  7.6 0.2 convolution_convert_fusion
  7.7 0.1 broadcast_divide_fusion
  7.8 0.1 slice_reduce_fusion
  7.9 0.2 fusion.42
  8.1 0.1 fusion.1
  8.2 0.1 broadcast_in_dim.17
  8.3 0.1 fusion.36
  8.4 0.7 pad_maximum_fusion.1.refs_4_
  9.1 0.1 copy.17
  9.1 0.4 fusion.44
  9.6 0.2 convolution_convert_fusion.1
  9.8 0.1 broadcast_divide_fusion.1
  9.8 0.1 slice_reduce_fusion.1
  10.0 0.2 fusion.43
  10.2 0.1 fusion
  10.3 0.1 broadcast_in_dim.15
  10.4 0.1 fusion.33
  10.5 0.7 pad_maximum_fusion.refs_3_
  11.1 0.1 copy.16
  11.2 0.0 copy-done.7
  11.2 0.0 copy-start.4
  11.2 0.0 copy-start.5
  11.3 0.7 copy-done.3
  11.9 0.0 copy-done.4
  12.0 0.0 copy-done.5
  12.0 134.9 %shard_map.111 = (bf16[2,4,6,1536]{3,2,1,0:T(8,128)(2,1)S(1)}, bf16[1536,256]{1,0:T(8,128)(2,1)S(1)}, bf16[256,1536]{1,0:T(8,128)(2,1)S(1)}, f32[4,8,1536]{2,1,0:T(8,128)S(1)}) custom-call(bf16[1536,256]{1,0:T(8,128)(2,1)S(1)} %bitcast.95, bf16[256,1536]{1,0:T(8,128)(2,1)S(1)} %bitcast.96, bf16[4,2,1536]{2,1,0:T(2,128)(2,1)S(1)} %bitcast.101, ...), custom_call_target="tpu_custom_call" | custom-call | tf_op jit(solution)/shard_map/pallas_call | solution.py:466
  146.9 0.1 copy.18
  146.9 0.7 reshape.135
  147.7 0.9 copy.34
  148.5 0.9 copy.35
  149.4 0.7 copy.36
  (21 shorter events, 0.1 us)
Async XLA Ops:
  0.6 0.7 copy-start.9
  3.2 0.7 copy-start.8
  4.4 1.7 %copy-start.6 = (bf16[1,2,6,6144]{3,1,2,0:T(2,128)(2,1)S(1)}, bf16[1,2,6,6144]{3,1,2,0:T(2,128)(2,1)}, u32[]{:S(2)}) copy-start(bf16[1,2,6,6144]{3,1,2,0:T(2,128)(2,1)} %param.8) | copy-start | bytes 442372
  6.2 0.9 copy-start
  7.1 4.1 %copy-start.7 = (bf16[6,6144]{1,0:T(8,128)(2,1)S(1)}, bf16[6,6144]{1,0:T(8,128)(2,1)}, u32[]{:S(2)}) copy-start(bf16[6,6144]{1,0:T(8,128)(2,1)} %param.10) | copy-start | bytes 221188
  7.1 4.2 %copy-start.2 = (bf16[1,1,256,1536]{3,2,1,0:T(8,128)(2,1)S(1)}, bf16[1,1,256,1536]{3,2,1,0:T(8,128)(2,1)}, u32[]{:S(2)}) copy-start(bf16[1,1,256,1536]{3,2,1,0:T(8,128)(2,1)} %param.15) | copy-start | bytes 2359300
  7.5 3.7 %copy-start.1 = (bf16[1,1,1536,256]{3,2,1,0:T(8,128)(2,1)S(1)}, bf16[1,1,1536,256]{3,2,1,0:T(8,128)(2,1)}, u32[]{:S(2)}) copy-start(bf16[1,1,1536,256]{3,2,1,0:T(8,128)(2,1)} %param.14) | copy-start | bytes 2359300
  11.2 0.7 copy-start.3
  11.2 0.8 copy-start.4
  11.2 0.8 copy-start.5

commit v5 on v3

--- a/solution.py
+++ b/solution.py
@@ -199,10 +199,9 @@
             g.x_pass()
         for g in now:
             g.x_wait()
-        if first_step:
-            later.z_wait()
-            later.x_start()
-
+
+        if not first_step:
+            later.x_wait()
         xmat = xs[:, :, :, 0:part].reshape(256, part)
         pu, ra, sb, rb, dd = local_ref("pu"), local_ref("ra"), local_ref("sb"), local_ref("rb"), local_ref("dd")
         pre = jnp.dot(xmat, w_in[...], preferred_element_type=f32)
@@ -215,8 +214,6 @@
         copy(pu.at[pl.ds(2 * (1 - core), 2)], ra, s1, core_dev).wait_recv()
         sb[...] = pu[pl.ds(2 * core, 2)] + ra[...]
         go(sb.at[1 - odd], rb, s2, odd_dev)
-        if first_step:
-            later.x_pass()
         copy(sb.at[1 - odd], rb, s2, odd_dev).wait_recv()
         k = 2 * core + odd
         both = sb[odd] + rb[...]
@@ -255,8 +252,6 @@
         def piece(top, x):
             return dx.at[pl.ds(2 * top, 2), x]
 
-        if first_step:
-            later.x_wait()
         b = slots(6)
         go(piece(0, across), ry.at[0], b[0], x_dev(1))
         go(piece(1, across), ry.at[1], b[1], x_dev(3))
@@ -308,6 +303,9 @@
         e = slots(3)
         for r in range(1, 4):
             go(dz.at[(zpos + r) % 4], rz.at[r - 1], e[r - 1], z_dev(r))
+        if first_step:
+            later.z_wait()
+            later.x_start()
         copy(ah.at[half], ah.at[1 - half], sh, half_dev).wait_recv()
         dgate = (ah[0] + ah[1])[0:1]
         ext = jnp.transpose(xs[:, :, :, part:wide].reshape(256, EXT).astype(f32))
@@ -342,6 +340,8 @@
         n = slots(7)
         for r in range(1, 8):
             go(split.at[(line + r) % 8], rf.at[line], n[r - 1], near_dev(r))
+        if first_step:
+            later.x_pass()
         stay.wait()
         for r in range(1, 8):
             copy(split.at[0], rf.at[(line + 8 - r) % 8], n[r - 1], near_dev(r)).wait_recv()

time: 148 us -> 148 us (level); the launches traced: 147 us -> 149 us
    pallas_call x1, Pallas kernels: 132 us -> 133 us  [run_window(): pl.pallas_call(functools.partial(window_kernel, part, hidden, experts, se...]
where the time goes in v5:
time: 148 us; the launch traced here: 149 us
  Pallas kernels  133 us (90%)
  local copies, waits for them, and re-layouts  7.34 us (5%)
  other arithmetic  3.17 us (2%)
  matrix products  2.62 us (2%)
  between operations  2.1 us (1%)
    pallas_call x1, Pallas kernels, run_window(): pl.pallas_call(functools.partial(window_kernel, part, hidden, experts, se...  133 us
    unnamed x23, local copies, waits for them, and re-layouts  5.18 us

profile of v5, /device:TPU:1, one launch (start us, length us, event | category | flops | bytes accessed | tf_op | source)
XLA Modules:
  0.0 148.5 jit_solution(16976210677729922481)
XLA Ops:
  0.6 0.0 copy-start.9
  0.6 0.6 copy-done.9
  1.3 0.6 dynamic_slice.3
  3.2 0.0 copy-start.8
  3.2 0.7 copy-done.8
  3.9 0.2 reduce-window.17
  4.1 0.2 reduce-window.16
  4.3 0.1 fusion.13
  4.3 0.1 fusion.14
  4.4 0.0 copy-start.6
  4.5 0.9 broadcast_select_fusion
  5.4 0.8 convolution_convert_fusion.2
  6.2 0.0 copy-done.6
  6.2 0.2 fusion.41
  6.4 0.7 copy-done
  7.1 0.4 fusion.45
  7.5 0.0 copy-start.1
  7.6 0.2 convolution_convert_fusion
  7.7 0.1 broadcast_divide_fusion
  7.8 0.1 slice_reduce_fusion
  7.9 0.2 fusion.42
  8.1 0.1 fusion.1
  8.2 0.1 broadcast_in_dim.17
  8.3 0.1 fusion.36
  8.4 0.7 pad_maximum_fusion.1.refs_4_
  9.1 0.1 copy.17
  9.1 0.4 fusion.44
  9.6 0.2 convolution_convert_fusion.1
  9.8 0.1 broadcast_divide_fusion.1
  9.8 0.1 slice_reduce_fusion.1
  10.0 0.2 fusion.43
  10.2 0.1 fusion
  10.3 0.1 broadcast_in_dim.15
  10.4 0.1 fusion.33
  10.5 0.7 pad_maximum_fusion.refs_3_
  11.1 0.1 copy.16
  11.2 0.0 copy-done.7
  11.2 0.0 copy-start.4
  11.2 0.0 copy-start.5
  11.3 0.7 copy-done.3
  11.9 0.0 copy-done.4
  12.0 0.0 copy-done.5
  12.0 133.3 %shard_map.111 = (bf16[2,4,6,1536]{3,2,1,0:T(8,128)(2,1)S(1)}, bf16[1536,256]{1,0:T(8,128)(2,1)S(1)}, bf16[256,1536]{1,0:T(8,128)(2,1)S(1)}, f32[4,8,1536]{2,1,0:T(8,128)S(1)}) custom-call(bf16[1536,256]{1,0:T(8,128)(2,1)S(1)} %bitcast.95, bf16[256,1536]{1,0:T(8,128)(2,1)S(1)} %bitcast.96, bf16[4,2,1536]{2,1,0:T(2,128)(2,1)S(1)} %bitcast.101, ...), custom_call_target="tpu_custom_call" | custom-call | tf_op jit(solution)/shard_map/pallas_call | solution.py:432
  145.3 0.1 copy.18
  145.4 0.7 reshape.135
  146.1 0.9 copy.34
  147.0 0.9 copy.35
  147.8 0.7 copy.36
  (21 shorter events, 0.1 us)
Async XLA Ops:
  0.6 0.7 copy-start.9
  3.2 0.7 copy-start.8
  4.4 1.7 %copy-start.6 = (bf16[1,2,6,6144]{3,1,2,0:T(2,128)(2,1)S(1)}, bf16[1,2,6,6144]{3,1,2,0:T(2,128)(2,1)}, u32[]{:S(2)}) copy-start(bf16[1,2,6,6144]{3,1,2,0:T(2,128)(2,1)} %param.8) | copy-start | bytes 442372
  6.2 0.9 copy-start
  7.1 4.1 %copy-start.7 = (bf16[6,6144]{1,0:T(8,128)(2,1)S(1)}, bf16[6,6144]{1,0:T(8,128)(2,1)}, u32[]{:S(2)}) copy-start(bf16[6,6144]{1,0:T(8,128)(2,1)} %param.10) | copy-start | bytes 221188
  7.1 4.2 %copy-start.2 = (bf16[1,1,256,1536]{3,2,1,0:T(8,128)(2,1)S(1)}, bf16[1,1,256,1536]{3,2,1,0:T(8,128)(2,1)}, u32[]{:S(2)}) copy-start(bf16[1,1,256,1536]{3,2,1,0:T(8,128)(2,1)} %param.15) | copy-start | bytes 2359300
  7.5 3.7 %copy-start.1 = (bf16[1,1,1536,256]{3,2,1,0:T(8,128)(2,1)S(1)}, bf16[1,1,1536,256]{3,2,1,0:T(8,128)(2,1)}, u32[]{:S(2)}) copy-start(bf16[1,1,1536,256]{3,2,1,0:T(8,128)(2,1)} %param.14) | copy-start | bytes 2359300
  11.2 0.7 copy-start.3
  11.2 0.8 copy-start.4
  11.2 0.8 copy-start.5
